TPU v7x, 32 devices: a whole 2x2x4 slice. The times are simulated.
32 devices in a mesh: wide: 16 (over z, x, core), depth: 2 (over y).
Axes of the slice: x: 2, y: 2, z: 4, core: 2. Of those that a mesh axis runs over, the one named last changes fastest.
Arguments:
- schur: float32 [16, 2, 1536, 1536], P('wide', 'depth'), as said below
- loads: float32 [16, 2, 1536, 128], P('wide', 'depth'), may hold values from -6 to 6
- face_sizes: int32 [16, 2, 6], P('wide', 'depth'), may hold values from 64 to 256, as said below
- face_dir: int32 [16, 2, 6], P('wide', 'depth'), may hold values from 0 to 5, as said below
Outputs:
- displacement: float32 [16, 2, 1536, 128], P('wide', 'depth')
- residual: float32 [16, 2, 1536, 128], P('wide', 'depth')
Inputs may be any that keep to these rules, and one draw needn't show every extreme that they name: `face_sizes`: A face slot and the neighbour's slot facing back across the same face have the same size; some slot holds 256 used unknowns and some holds 64. `face_dir`: each subdomain's six entries are 0 to 5 in some order: 0 faces the lower neighbour along wide, 1 the upper one, 2 the lower neighbour along depth, 3 the upper one, 4 and 5 the supported top and bottom surfaces. `schur`: each subdomain's matrix is symmetric and positive definite.
All inputs are finite; a program needn't handle non-finite values.
Results may differ from a plain program's by a relative error of at most 0.00017.
Values sent between devices are 32-bit elements; how exact they have to be, the bound alone decides.
No kernel may reach another device: no remote copies, remote signals or barrier semaphores. Data moves between devices by JAX's collectives and lax.ppermute only.
A program may use at most 128 MiB of HBM per device.

v0:
```python
import jax
import jax.numpy as jnp
from jax import lax
from jax.sharding import PartitionSpec as P

ITERS = 2


OMEGA = 0.6


def from_behind(value, axis, steps):
    count = lax.axis_size(axis)
    first, last = (max(0, -steps), min(count, count - steps))
    return lax.ppermute(value, axis, [(source, source + steps) for source in range(first, last)])


def assemble(select, parts):
    facing = jnp.einsum("kd,kfr->dfr", select, parts, precision=lax.Precision.HIGHEST)
    from_lower_w = from_behind(facing[1], "wide", 1)
    from_upper_w = from_behind(facing[0], "wide", -1)
    from_lower_d = from_behind(facing[3], "depth", 1)
    from_upper_d = from_behind(facing[2], "depth", -1)
    blank = jnp.zeros_like(facing[0])
    arrived = jnp.stack(
        [from_lower_w, from_upper_w, from_lower_d, from_upper_d, blank, blank], axis=0
    )
    return parts + jnp.einsum("kd,dfr->kfr", select, arrived, precision=lax.Precision.HIGHEST)


def local(schur, loads, face_sizes, face_dir):
    matrix = schur[0, 0]
    load = loads[0, 0]
    sizes = face_sizes[0, 0]
    dirs = face_dir[0, 0]
    order_rows = matrix.shape[0]
    slot_rows = order_rows // 6
    cases = load.shape[1]
    mask = (jnp.arange(slot_rows, dtype=jnp.int32)[None, :] < sizes[:, None]).astype(jnp.float32)
    select = (dirs[:, None] == jnp.arange(6, dtype=jnp.int32)[None, :]).astype(jnp.float32)
    shaped = matrix.reshape(6, slot_rows, 6, slot_rows)
    blocks = jnp.stack([shaped[k, :, k, :] for k in range(6)], axis=0)
    first = load.reshape(6, slot_rows, cases) * mask[:, :, None]
    summed = assemble(select, blocks)
    resid = assemble(select, first)
    ident = jnp.eye(slot_rows, dtype=jnp.float32)
    summed = summed * mask[:, :, None] * mask[:, None, :] + ident * (1.0 - mask[:, :, None])
    factor = jnp.linalg.cholesky(summed)
    inverse = jax.scipy.linalg.cho_solve((factor, True), jnp.broadcast_to(ident, summed.shape))

    def partial_value(disp):
        applied = jnp.dot(matrix, disp.reshape(order_rows, cases), precision=lax.Precision.HIGHEST)
        return (load - applied).reshape(6, slot_rows, cases) * mask[:, :, None]

    disp = jnp.zeros((6, slot_rows, cases), jnp.float32)
    for step in range(ITERS):
        if step > 0:
            resid = assemble(select, partial_value(disp))
        update = jnp.einsum("kfg,kgc->kfc", inverse, resid, precision=lax.Precision.HIGHEST)
        disp = disp + OMEGA * update
    final = assemble(select, partial_value(disp))
    return (disp.reshape(1, 1, order_rows, cases), final.reshape(1, 1, order_rows, cases))


def solution(mesh):
    return jax.shard_map(
        local,
        mesh=mesh,
        in_specs=(
            P("wide", "depth", None, None),
            P("wide", "depth", None, None),
            P("wide", "depth", None),
            P("wide", "depth", None),
        ),
        out_specs=(P("wide", "depth", None, None), P("wide", "depth", None, None)),
        check_vma=False,
    )
```

profile of v0, /device:TPU:8, one launch (start us, length us, event | category | flops | bytes accessed | tf_op | source)
XLA Modules:
  0.0 505.3 jit_solution(12225048625623669507)
XLA Ops:
  0.6 12.0 %reshape_squeeze.6 = f32[6,256,6,256]{3,2,1,0:T(8,128)} reshape(f32[1,1,1536,1536]{3,2,1,0:T(8,128)} %param.4) | data formatting | bytes 18874368 | tf_op jit(solution)/shard_map/reshape;squeeze | solution.py:41
  12.6 6.3 %fusion.60 = (f32[1,256,1,256]{3,2,1,0:T(1,128)S(1)}, f32[1,256,1,256]{3,2,1,0:T(1,128)S(1)}, f32[1,256,1,256]{3,2,1,0:T(1,128)S(1)}, f32[1,256,1,256]{3,2,1,0:T...) fusion(f32[6,256,6,256]{3,2,1,0:T(8,128)} %reshape_squeeze.6), kind=kLoop, calls=%fused_computation.88 | loop fusion | bytes 3145728 | tf_op jit(solution)/shard_map/slice | solution.py:42
  24.1 2.1 copy.93
  26.3 1.4 fusion.42
  28.5 1.9 collective-permute-start
  33.1 3.5 collective-permute-start.4
  36.6 3.0 collective-permute-start.5
  39.6 3.4 collective-permute-start.6
  50.9 2.1 collective-permute-start.1
  53.1 5.1 %collective-permute-start.2 = (f32[256,256]{1,0:T(8,128)}, f32[256,256]{1,0:T(8,128)}, u32[]{:S(2)}, u32[]{:S(2)}) collective-permute-start(f32[256,256]{1,0:T(8,128)} %bitcast.164), channel_id=1, source_target_pairs={{0,1},{2,3},{4,5},{6,7},{8,9},{10,11},{12,13},{14,15},{16,17},{18,... | collective-permute-start | bytes 786440 | tf_op jit(solution)/shard_map/ppermute | solution.py:15
  58.1 1.5 collective-permute-start.3
  60.4 2.4 stack.77
  62.8 2.7 convolution_add_fusion.2
  67.0 1.9 copy.96
  69.0 1.9 copy.97
  71.0 4.4 stack.72
  75.4 3.1 fusion.47
  78.5 1.8 copy.98
  80.3 1.8 multiply_add_fusion
  84.1 71.0 %custom-call.20 = f32[6,128,128]{2,1,0:T(8,128)} custom-call(f32[6,128,128]{2,1,0:T(8,128)S(1)} %cholesky.122), custom_call_target="Cholesky" | custom-call | tf_op jit(solution)/shard_map/jit(cholesky)/cholesky | solution.py:48
  157.1 60.8 %custom-call.21 = f32[6,1,128,128]{2,3,1,0:T(8,128)} custom-call(f32[6,1,128,128]{3,2,1,0:T(8,128)} %select_bitcast_fusion), custom_call_target="InvertDiagBlocksLowerTriangular" | custom-call | tf_op jit(solution)/shard_map/jit(cholesky)/cholesky | solution.py:48
  217.9 1.5 constant_dynamic-update-slice_fusion.1
  219.4 1.7 convolution_subtract_fusion.2
  221.1 71.1 %custom-call.22 = f32[6,128,128]{2,1,0:T(8,128)S(1)} custom-call(f32[6,128,128]{2,1,0:T(8,128)} %convolution_subtract_fusion.2), custom_call_target="Cholesky" | custom-call | tf_op jit(solution)/shard_map/jit(cholesky)/cholesky | solution.py:48
  294.5 1.7 select_select_fusion
  296.3 5.7 %while.1 = (s32[]{:T(128)}, f32[6,256,256]{2,1,0:T(8,128)S(1)}, s32[2,2]{1,0:T(2,128)S(1)}, f32[2,6,128,128]{3,2,0,1:T(8,128)}, s32[]{:T(128)}) while((s32[]{:T(128)}, f32[6,256,256]{2,1,0:T(8,128)S(1)}, s32[2,2]{1,0:T(2,128)S(1)}, f32[2,6,128,128]{3,2,0,1:T(8,128)}, s32[]{:T(128)}) %tuple.45), condition=%wide.while_cond, body=%wide.while_body.sunk | while | flops 2 | bytes 788065 | solution.py:49
  297.0 2.2 bitcast_dynamic-update-slice_fusion.8
  299.8 2.2 bitcast_dynamic-update-slice_fusion.8
  302.0 118.9 %custom-call.23 = f32[6,2,128,128]{2,3,1,0:T(8,128)S(1)} custom-call(f32[6,2,128,128]{3,2,1,0:T(8,128)} %bitcast.214), custom_call_target="InvertDiagBlocksLowerTriangular" | custom-call | tf_op jit(solution)/shard_map/jit(_cho_solve)/vmap()/triangular_solve | solution.py:49
  421.8 1.9 fusion.29
  423.7 1.8 convolution_subtract_fusion.1
  425.5 1.9 fusion.33
  430.7 1.6 convolution_multiply_fusion.1
  432.4 11.0 %fusion.7 = f32[1536,128]{0,1:T(8,128)} fusion(f32[1536,128]{1,0:T(8,128)S(1)} %bitcast.181, f32[1,1,1536,1536]{3,2,1,0:T(8,128)S(1)} %bitcast.174, f32[1,1,1536,128]{2,3,1,0:T(8,128)S(1)} %copy-done.1), kind=kOutput, calls=%fused_computation.7 | convolution fusion | flops 3624075264 | bytes 11796480 | tf_op jit(solution)/shard_map/dot_general | solution.py:52
  443.4 1.4 copy.117
  446.5 2.1 collective-permute-start.8
  448.6 4.3 collective-permute-start.9
  453.0 5.9 %collective-permute-start.10 = (f32[256,128]{1,0:T(8,128)S(1)}, f32[256,128]{1,0:T(8,128)}, u32[]{:S(2)}, u32[]{:S(2)}) collective-permute-start(f32[256,128]{1,0:T(8,128)S(1)} %bitcast.198), channel_id=1, source_target_pairs={{0,1},{2,3},{4,5},{6,7},{8,9},{10,11},{12,13},{14,15},{16,17},{18,... | collective-permute-start | bytes 393224 | tf_op jit(solution)/shard_map/ppermute | solution.py:15
  460.7 5.1 %collective-permute-done.11 = f32[256,128]{1,0:T(8,128)} collective-permute-done((f32[256,128]{1,0:T(8,128)S(1)}, f32[256,128]{1,0:T(8,128)}, u32[]{:S(2)}, u32[]{:S(2)}) %collective-permute-start.11) | collective-permute-done | bytes 131104 | tf_op jit(solution)/shard_map/ppermute | solution.py:15
  465.8 3.5 stack.82
  469.3 2.4 convolution_add_fusion.1
  471.7 1.7 fusion.17
  474.2 10.8 %fusion.13 = f32[1536,128]{0,1:T(8,128)S(1)} fusion(f32[1536,128]{1,0:T(8,128)S(1)} %bitcast.182, f32[1,1,1536,1536]{3,2,1,0:T(8,128)} %param.4, f32[1,1,1536,128]{2,3,1,0:T(8,128)S(1)} %copy-done.1), kind=kOutput, calls=%fused_computation.9 | convolution fusion | flops 3624075264 | bytes 11796480 | tf_op jit(solution)/shard_map/dot_general | solution.py:52
  485.3 1.3 fusion.18
  487.0 1.9 collective-permute-start.12
  488.9 4.5 collective-permute-start.13
  493.5 1.4 collective-permute-start.14
  497.4 4.4 collective-permute-done.15
  (127 shorter events, 41.3 us)
Async XLA Ops:
  24.1 2.1 copy-start.18
  27.7 2.8 copy-start.20
  27.7 3.0 copy-start
  28.5 37.0 %collective-permute-start = (f32[256,256]{1,0:T(8,128)S(1)}, f32[256,256]{1,0:T(8,128)S(1)}, u32[]{:S(2)}, u32[]{:S(2)}) collective-permute-start(f32[256,256]{1,0:T(8,128)S(1)} %bitcast.185), channel_id=1, source_target_pairs={{0,2},{2,4},{4,6},{6,8},{8,10},{10,12},{12,14},{14,16},{16,18},{18... | collective-permute-start | bytes 786440 | tf_op jit(solution)/shard_map/ppermute | solution.py:15
  33.1 17.8 %collective-permute-start.4 = (f32[256,128]{1,0:T(8,128)}, f32[256,128]{1,0:T(8,128)S(1)}, u32[]{:S(2)}, u32[]{:S(2)}) collective-permute-start(f32[256,128]{1,0:T(8,128)} %bitcast.23), channel_id=1, source_target_pairs={{0,2},{2,4},{4,6},{6,8},{8,10},{10,12},{12,14},{14,16},{16,18},{18... | collective-permute-start | bytes 393224 | tf_op jit(solution)/shard_map/ppermute | solution.py:15
  36.6 16.4 %collective-permute-start.5 = (f32[256,128]{1,0:T(8,128)}, f32[256,128]{1,0:T(8,128)S(1)}, u32[]{:S(2)}, u32[]{:S(2)}) collective-permute-start(f32[256,128]{1,0:T(8,128)} %bitcast.26), channel_id=1, source_target_pairs={{2,0},{4,2},{6,4},{8,6},{10,8},{12,10},{14,12},{16,14},{18,16},{20... | collective-permute-start | bytes 393224 | tf_op jit(solution)/shard_map/ppermute | solution.py:15
  39.6 18.5 %collective-permute-start.6 = (f32[256,128]{1,0:T(8,128)}, f32[256,128]{1,0:T(8,128)S(1)}, u32[]{:S(2)}, u32[]{:S(2)}) collective-permute-start(f32[256,128]{1,0:T(8,128)} %bitcast.29), channel_id=1, source_target_pairs={{0,1},{2,3},{4,5},{6,7},{8,9},{10,11},{12,13},{14,15},{16,17},{18,... | collective-permute-start | bytes 393224 | tf_op jit(solution)/shard_map/ppermute | solution.py:15
  43.0 16.6 %collective-permute-start.7 = (f32[256,128]{1,0:T(8,128)}, f32[256,128]{1,0:T(8,128)S(1)}, u32[]{:S(2)}, u32[]{:S(2)}) collective-permute-start(f32[256,128]{1,0:T(8,128)} %bitcast.32), channel_id=1, source_target_pairs={{1,0},{3,2},{5,4},{7,6},{9,8},{11,10},{13,12},{15,14},{17,16},{19,... | collective-permute-start | bytes 393224 | tf_op jit(solution)/shard_map/ppermute | solution.py:15
  50.9 14.9 %collective-permute-start.1 = (f32[256,256]{1,0:T(8,128)S(1)}, f32[256,256]{1,0:T(8,128)}, u32[]{:S(2)}, u32[]{:S(2)}) collective-permute-start(f32[256,256]{1,0:T(8,128)S(1)} %bitcast.187), channel_id=1, source_target_pairs={{2,0},{4,2},{6,4},{8,6},{10,8},{12,10},{14,12},{16,14},{18,16},{20... | collective-permute-start | bytes 786440 | tf_op jit(solution)/shard_map/ppermute | solution.py:15
  53.1 14.0 %collective-permute-start.2 = (f32[256,256]{1,0:T(8,128)}, f32[256,256]{1,0:T(8,128)}, u32[]{:S(2)}, u32[]{:S(2)}) collective-permute-start(f32[256,256]{1,0:T(8,128)} %bitcast.164), channel_id=1, source_target_pairs={{0,1},{2,3},{4,5},{6,7},{8,9},{10,11},{12,13},{14,15},{16,17},{18,... | collective-permute-start | bytes 786440 | tf_op jit(solution)/shard_map/ppermute | solution.py:15
  58.1 1.5 copy-start.14
  58.1 10.8 %collective-permute-start.3 = (f32[256,256]{1,0:T(8,128)}, f32[256,256]{1,0:T(8,128)}, u32[]{:S(2)}, u32[]{:S(2)}) collective-permute-start(f32[256,256]{1,0:T(8,128)} %bitcast.163), channel_id=1, source_target_pairs={{1,0},{3,2},{5,4},{7,6},{9,8},{11,10},{13,12},{15,14},{17,16},{19,... | collective-permute-start | bytes 786440 | tf_op jit(solution)/shard_map/ppermute | solution.py:15
  59.6 0.7 copy-start.15
  60.4 5.1 %copy-start.7 = (f32[2,256,128]{2,0,1:T(2,128)}, f32[2,256,128]{2,0,1:T(2,128)S(1)}, u32[]{:S(2)}) copy-start(f32[2,256,128]{2,0,1:T(2,128)S(1)} %broadcast.167) | copy-start | bytes 786436
  82.8 1.2 copy-start.5
  84.0 72.2 %copy-start.17 = (pred[128,128]{1,0:T(8,128)(4,1)S(1)}, pred[128,128]{1,0:T(8,128)(4,1)}, u32[]{:S(2)}) copy-start(pred[128,128]{1,0:T(8,128)(4,1)} %iota_compare_fusion.2) | copy-start | bytes 49156
  84.1 133.8 %copy-start.6 = (f32[6,256,256]{2,1,0:T(8,128)S(1)}, f32[6,256,256]{2,1,0:T(8,128)}, u32[]{:S(2)}) copy-start(f32[6,256,256]{2,1,0:T(8,128)} %copy-done.5) | copy-start | bytes 4718596
  155.1 1.2 copy-start.9
  217.9 74.4 %copy-start.16 = (pred[128,128]{1,0:T(8,128)(4,1)S(1)}, pred[128,128]{1,0:T(8,128)(4,1)}, u32[]{:S(2)}) copy-start(pred[128,128]{1,0:T(8,128)(4,1)} %iota_compare_fusion.3) | copy-start | bytes 49156
  293.3 1.2 copy-start.4
  294.5 1.8 copy-start.21
  294.5 137.9 %slice-start = ((s8[9437184]{0:T(1024)(128)(4,1)}), s8[1048576]{0:T(1024)(128)(4,1)S(1)}, s32[]{:S(2)}) async-start(s8[9437184]{0:T(1024)(128)(4,1)} %bitcast.173), calls=%async_computation | async-start | bytes 2097152
  420.9 0.9 copy-start.12
  421.8 10.6 %slice-start.1 = ((s8[9437184]{0:T(1024)(128)(4,1)}), s8[4194304]{0:T(1024)(128)(4,1)S(1)}, s32[]{:S(2)}) async-start(s8[9437184]{0:T(1024)(128)(4,1)} %bitcast.173), calls=%async_computation.1 | async-start | bytes 8388608
  423.7 3.7 copy-start.13
  427.4 3.4 copy-start.10
  428.2 4.2 slice-start.2
  429.9 0.9 copy-start.2
  430.7 1.6 copy-start.1
  443.4 1.4 copy-start.19
  444.8 21.0 %copy-start.8 = (f32[2,256,128]{2,0,1:T(2,128)S(1)}, f32[2,256,128]{2,0,1:T(2,128)}, u32[]{:S(2)}) copy-start(f32[2,256,128]{2,0,1:T(2,128)} %copy-done.7) | copy-start | bytes 786436
  446.5 13.7 %collective-permute-start.8 = (f32[256,128]{1,0:T(8,128)S(1)}, f32[256,128]{1,0:T(8,128)}, u32[]{:S(2)}, u32[]{:S(2)}) collective-permute-start(f32[256,128]{1,0:T(8,128)S(1)} %bitcast.202), channel_id=1, source_target_pairs={{0,2},{2,4},{4,6},{6,8},{8,10},{10,12},{12,14},{14,16},{16,18},{18... | collective-permute-start | bytes 393224 | tf_op jit(solution)/shard_map/ppermute | solution.py:15
  448.6 11.5 %collective-permute-start.9 = (f32[256,128]{1,0:T(8,128)S(1)}, f32[256,128]{1,0:T(8,128)}, u32[]{:S(2)}, u32[]{:S(2)}) collective-permute-start(f32[256,128]{1,0:T(8,128)S(1)} %bitcast.200), channel_id=1, source_target_pairs={{2,0},{4,2},{6,4},{8,6},{10,8},{12,10},{14,12},{16,14},{18,16},{20... | collective-permute-start | bytes 393224 | tf_op jit(solution)/shard_map/ppermute | solution.py:15
  453.0 7.7 %collective-permute-start.10 = (f32[256,128]{1,0:T(8,128)S(1)}, f32[256,128]{1,0:T(8,128)}, u32[]{:S(2)}, u32[]{:S(2)}) collective-permute-start(f32[256,128]{1,0:T(8,128)S(1)} %bitcast.198), channel_id=1, source_target_pairs={{0,1},{2,3},{4,5},{6,7},{8,9},{10,11},{12,13},{14,15},{16,17},{18,... | collective-permute-start | bytes 393224 | tf_op jit(solution)/shard_map/ppermute | solution.py:15
  458.9 7.0 %collective-permute-start.11 = (f32[256,128]{1,0:T(8,128)S(1)}, f32[256,128]{1,0:T(8,128)}, u32[]{:S(2)}, u32[]{:S(2)}) collective-permute-start(f32[256,128]{1,0:T(8,128)S(1)} %bitcast.196), channel_id=1, source_target_pairs={{1,0},{3,2},{5,4},{7,6},{9,8},{11,10},{13,12},{15,14},{17,16},{19,... | collective-permute-start | bytes 393224 | tf_op jit(solution)/shard_map/ppermute | solution.py:15
  469.3 2.4 copy-start.3
  473.4 0.9 copy-start.11
  487.0 9.2 %collective-permute-start.12 = (f32[256,128]{1,0:T(8,128)S(1)}, f32[256,128]{1,0:T(8,128)S(1)}, u32[]{:S(2)}, u32[]{:S(2)}) collective-permute-start(f32[256,128]{1,0:T(8,128)S(1)} %bitcast.203), channel_id=1, source_target_pairs={{0,2},{2,4},{4,6},{6,8},{8,10},{10,12},{12,14},{14,16},{16,18},{18... | collective-permute-start | bytes 393224 | tf_op jit(solution)/shard_map/ppermute | solution.py:15
  488.9 7.3 %collective-permute-start.13 = (f32[256,128]{1,0:T(8,128)S(1)}, f32[256,128]{1,0:T(8,128)S(1)}, u32[]{:S(2)}, u32[]{:S(2)}) collective-permute-start(f32[256,128]{1,0:T(8,128)S(1)} %bitcast.201), channel_id=1, source_target_pairs={{2,0},{4,2},{6,4},{8,6},{10,8},{12,10},{14,12},{16,14},{18,16},{20... | collective-permute-start | bytes 393224 | tf_op jit(solution)/shard_map/ppermute | solution.py:15
  493.5 3.9 collective-permute-start.14
  494.9 6.9 %collective-permute-start.15 = (f32[256,128]{1,0:T(8,128)S(1)}, f32[256,128]{1,0:T(8,128)S(1)}, u32[]{:S(2)}, u32[]{:S(2)}) collective-permute-start(f32[256,128]{1,0:T(8,128)S(1)} %bitcast.197), channel_id=1, source_target_pairs={{1,0},{3,2},{5,4},{7,6},{9,8},{11,10},{13,12},{15,14},{17,16},{19,... | collective-permute-start | bytes 393224 | tf_op jit(solution)/shard_map/ppermute | solution.py:15
where the time goes:
time: 514 us; the launch traced here: 505 us
  other arithmetic  330 us (64%)
  local copies, waits for them, and re-layouts  66.8 us (13%)
  matrix products  50.8 us (10%)
  starting transfers between devices  44.5 us (9%)
  waiting for transfers between devices  11.2 us (2%)
    another operation x9, other arithmetic, local(): factor = jnp.linalg.cholesky(summed)  206 us
    another operation x4, other arithmetic, local(): jax.scipy.linalg.cho_solve((factor, True), jnp.broadcast_to(ident, summed...  122 us
    ppermute x16, starting transfers between devices, from_behind(): lax.ppermute(value, axis, [(source, source + steps) for source in range(f...  44.5 us
    dot_general x2, matrix products, partial_value(): jnp.dot(matrix, disp.reshape(order_rows, cases), precision=lax.Precision....  21.8 us
    another operation x9, local copies, waits for them, and re-layouts, assemble(): jnp.stack([from_lower_w, from_upper_w, from_lower_d, from_upper_d, blank,...  16.7 us
    unnamed x66, local copies, waits for them, and re-layouts  12.6 us
    another operation x1, local copies, waits for them, and re-layouts, local(): shaped = matrix.reshape(6, slot_rows, 6, slot_rows)  12 us
    ppermute x16, waiting for transfers between devices, from_behind(): lax.ppermute(value, axis, [(source, source + steps) for source in range(f...  11.2 us
  transfers between devices with their start and end apart: 16, of which 4 were waited for; matrix products, arithmetic and copies ran while one was open for 4% of the time, Pallas kernels for 0%

commit v1 on v0

v1 whole, which is shorter than its diff:
```python
import functools

import jax
import jax.numpy as jnp
from jax import lax
from jax.experimental import pallas as pl
from jax.experimental.pallas import tpu as pltpu
from jax.sharding import PartitionSpec as P

ITERS = 2
OMEGA = 0.6

SLOTS = 6
LANES = 128
OUTER = 64
MICRO = 8
F32 = jnp.float32
BF16 = jnp.bfloat16
SMEM = pl.BlockSpec(memory_space=pltpu.SMEM)
VMEM = pl.BlockSpec(memory_space=pltpu.VMEM)
HBM = pl.BlockSpec(memory_space=pltpu.HBM)


def role_list(mesh):
    return [(axis, turn) for axis in ("wide", "depth") for turn in (0, 1) if mesh.shape[axis] > 1 + turn]


def role_slot(mesh, dirs_ref, role):
    axis, turn = role
    index = lax.axis_index(axis)
    count = mesh.shape[axis]
    upper = (index + turn) % 2 == 0
    facing = jnp.where(upper, 1, 0) + (0 if axis == "wide" else 2)
    slot = jnp.int32(0)
    for k in range(SLOTS):
        slot = slot + jnp.where(dirs_ref[k] == facing, k, 0)
    there = jnp.where(upper, index + 1 < count, index > 0)
    return slot, there


def exchange(mesh, role, value):
    axis, turn = role
    other = "depth" if axis == "wide" else "wide"
    count, rest = mesh.shape[axis], mesh.shape[other]
    pairs, left = [], []
    for line in range(rest):
        met = set()
        for low in range(turn, count - 1, 2):
            pairs.append(((low, line), (low + 1, line)))
            met |= {low, low + 1}
        left.append([(i, line) for i in range(count) if i not in met])
    alone = [spot for spots in left for spot in spots]
    pairs += list(zip(alone[::2], alone[1::2]))

    def flat(spot):
        place = {axis: spot[0], other: spot[1]}
        return place["wide"] * mesh.shape["depth"] + place["depth"]

    perm = []
    for one, two in pairs:
        perm += [(flat(one), flat(two)), (flat(two), flat(one))]
    return lax.ppermute(value, ("wide", "depth"), sorted(perm))


def spread_row(x, k):
    return jnp.broadcast_to(x[k : k + 1, :], x.shape)


def tree_sum(terms):
    while len(terms) > 1:
        terms = [terms[i] + terms[i + 1] if i + 1 < len(terms) else terms[i] for i in range(0, len(terms), 2)]
    return terms[0]


def invert_diagonal(d):
    rows, packs = len(d), len(d[0])
    lane = lax.broadcasted_iota(jnp.int32, (MICRO, LANES), 1)
    sub = lax.broadcasted_iota(jnp.int32, (MICRO, LANES), 0)
    half = lane & OUTER
    local = lane & (OUTER - 1)
    for q in range(rows):
        own = (local >= q * MICRO) & (local < (q + 1) * MICRO)
        spots = [half + (q * MICRO + j) for j in range(MICRO)]
        cols = [[jnp.take_along_axis(d[q][p], spots[j], axis=1) for j in range(MICRO)] for p in range(packs)]
        scales = [[None] * MICRO for _ in range(packs)]
        for k in range(MICRO):
            pivot_row = sub == k
            for p in range(packs):
                c = cols[p]
                scale = 1.0 / spread_row(c[k], k)
                scales[p][k] = scale
                h = jnp.where(pivot_row, 0.0, c[k]) * scale
                for j in range(MICRO):
                    if j != k:
                        c[j] = c[j] - h * spread_row(c[j], k)
                c[k] = jnp.where(pivot_row, 1.0, -h)
        for p in range(packs):
            scale = scales[p][0]
            for k in range(1, MICRO):
                scale = jnp.where(sub == k, scales[p][k], scale)
            row = jnp.where(own, jnp.where(local == sub + q * MICRO, 1.0, 0.0), d[q][p])
            row = tree_sum([cols[p][j] * spread_row(row, j) for j in range(MICRO)]) * scale
            spread = [spread_row(row, j) for j in range(MICRO)]
            for step in range(1, rows):
                i = (q + step) % rows
                x = d[i][p]
                change = tree_sum([jnp.take_along_axis(x, spots[j], axis=1) * spread[j] for j in range(MICRO)])
                d[i][p] = jnp.where(own, 0.0, x) - change
            d[q][p] = row
    return d


def split(x):
    high = x.astype(BF16)
    return high, (x - high.astype(F32)).astype(BF16)


def invert_blocks(a_ref):
    count, size = a_ref.shape[0], a_ref.shape[-1]
    lane = lax.broadcasted_iota(jnp.int32, (MICRO, LANES), 1)
    for block in range(size // OUTER):
        r0 = block * OUTER
        tile, h = divmod(r0, LANES)
        h //= OUTER
        tl = slice(tile * LANES, (tile + 1) * LANES)
        d = []
        for i in range(OUTER // MICRO):
            rows = slice(r0 + i * MICRO, r0 + (i + 1) * MICRO)
            line = []
            for p in range(count // 2):
                x, y = a_ref[2 * p, rows, tl], a_ref[2 * p + 1, rows, tl]
                if h == 0:
                    line.append(jnp.where(lane < OUTER, x, pltpu.roll(y, OUTER, 1)))
                else:
                    line.append(jnp.where(lane < OUTER, pltpu.roll(x, OUTER, 1), y))
            d.append(line)
        d = invert_diagonal(d)
        lane_row = lax.broadcasted_iota(jnp.int32, (OUTER, LANES), 1)
        own_row = (lane_row >= OUTER * h) & (lane_row < OUTER * (h + 1))
        lane_all = lax.broadcasted_iota(jnp.int32, (size, LANES), 1)
        own_all = (lane_all >= OUTER * h) & (lane_all < OUTER * (h + 1))
        for g in range(count):
            p, s = divmod(g, 2)
            w = jnp.concatenate([d[i][p] for i in range(OUTER // MICRO)], 0)
            if s != h:
                w = pltpu.roll(w, OUTER, 1)
            w = jnp.where(own_row, w, 0.0)
            w_high = w.astype(BF16)
            w_mixed = (w + pltpu.roll(w - w_high.astype(F32), OUTER, 1)).astype(BF16)
            high, low = split(a_ref[g, r0 : r0 + OUTER, :])
            zero = jnp.zeros_like(low)
            right = jnp.concatenate([high, high, low, zero] if h == 0 else [high, high, zero, low], 0)
            row = jnp.dot(jnp.concatenate([w_mixed, w_high], 1), right, preferred_element_type=F32)
            row = jnp.concatenate(
                [
                    jnp.where(own_row, w, row[:, c * LANES : (c + 1) * LANES]) if c == tile else row[:, c * LANES : (c + 1) * LANES]
                    for c in range(size // LANES)
                ],
                1,
            )
            column = a_ref[g, :, tl]
            c_high = column.astype(BF16)
            c_mixed = jnp.where(own_all, column, pltpu.roll(column - c_high.astype(F32), OUTER, 1)).astype(BF16)
            high, low = split(row)
            right = jnp.concatenate([high, high, low, zero] if h == 0 else [high, high, zero, low], 0)
            change = jnp.dot(jnp.concatenate([c_mixed, c_high], 1), right, preferred_element_type=F32)
            for c in range(size // LANES):
                cl = slice(c * LANES, (c + 1) * LANES)
                base = a_ref[g, :, cl]
                if c == tile:
                    base = jnp.where(own_all, 0.0, base)
                a_ref[g, :, cl] = base - change[:, cl]
            a_ref[g, r0 : r0 + OUTER, :] = row


def slot_rows(slot, rows):
    return pl.ds(pl.multiple_of(slot * rows, rows), rows)


def row_mask(rows, size, lanes=LANES):
    return lax.broadcasted_iota(jnp.int32, (rows, lanes), 0) < size


def pack_kernel(mesh, roles, dirs, sizes, matrix, loads, *rest):
    outs, (block, load, sems) = rest[: len(roles)], rest[len(roles) :]
    rows = block.shape[1]
    cases = load.shape[2]
    copies = []
    for n, role in enumerate(roles):
        slot, _ = role_slot(mesh, dirs, role)
        at = slot_rows(slot, rows)
        one = pltpu.make_async_copy(matrix.at[at, at], block.at[n], sems.at[n, 0])
        two = pltpu.make_async_copy(loads.at[at, :], load.at[n], sems.at[n, 1])
        one.start()
        two.start()
        copies.append((one, two, slot))
    for n, (one, two, slot) in enumerate(copies):
        one.wait()
        two.wait()
        outs[n][:, :rows] = block[n]
        outs[n][:, rows:] = jnp.where(row_mask(rows, sizes[slot], cases), load[n], 0.0)


def split_kernel(matrix, high_ref, low_ref, diagonal, buffer, sems):
    order = matrix.shape[0]
    rows = diagonal.shape[1]
    chunk = buffer.shape[1]
    total = order // chunk

    def copy(n):
        return pltpu.make_async_copy(matrix.at[pl.ds(n * chunk, chunk), :], buffer.at[n % 2], sems.at[n % 2])

    copy(0).start()
    for n in range(total):
        if n + 1 < total:
            copy(n + 1).start()
        copy(n).wait()
        x = buffer[n % 2]
        high, low = split(x)
        at = slice(n * chunk, (n + 1) * chunk)
        high_ref[at, :] = high
        low_ref[at, :] = low
        k, start = divmod(n * chunk, rows)
        diagonal[k, start : start + chunk, :] = buffer[n % 2, :, k * rows : (k + 1) * rows]


def inverse_kernel(mesh, roles, dirs, sizes, diagonal, *rest):
    got = rest[: len(roles)]
    high_ref, low_ref, work = rest[len(roles) :]
    rows = work.shape[-1]
    work[...] = diagonal[...]
    for n, role in enumerate(roles):
        slot, there = role_slot(mesh, dirs, role)
        work[slot] = work[slot] + jnp.where(there, 1.0, 0.0) * got[n][:, :rows]
    r = lax.broadcasted_iota(jnp.int32, (rows, rows), 0)
    c = lax.broadcasted_iota(jnp.int32, (rows, rows), 1)
    for k in range(SLOTS):
        used = jnp.maximum(r, c) < sizes[k]
        work[k] = jnp.where(used, work[k], jnp.where(r == c, 1.0, 0.0))
    invert_blocks(work)
    for k in range(SLOTS):
        high_ref[k], low_ref[k] = split(work[k])


def step_kernel(mesh, roles, first, dirs, sizes, s_high, s_low, i_high, i_low, loads, *rest):
    got, rest = rest[: len(roles)], rest[len(roles) :]
    if first:
        before = None
    else:
        (before, previous), rest = rest[:2], rest[2:]
    disp, part, rest = rest[0], rest[1], rest[2:]
    outs, (resid, pair) = rest[: len(roles)], rest[len(roles) :]
    rows, cases = i_high.shape[1], loads.shape[1]
    for k in range(SLOTS):
        at = slice(k * rows, (k + 1) * rows)
        if first:
            resid[at, :] = jnp.where(row_mask(rows, sizes[k], cases), loads[at, :], 0.0)
        else:
            resid[at, :] = previous[at, :]
    slots = [role_slot(mesh, dirs, role) for role in roles]
    for n, (slot, there) in enumerate(slots):
        at = slot_rows(slot, rows)
        here = got[n][:, got[n].shape[1] - cases :]
        resid[at, :] = resid[at, :] + jnp.where(there, 1.0, 0.0) * here
    for k in range(SLOTS):
        at = slice(k * rows, (k + 1) * rows)
        both = jnp.concatenate(split(resid[at, :]), 1)
        update = jnp.dot(i_high[k], both, preferred_element_type=F32)
        update += jnp.dot(i_low[k], both, preferred_element_type=F32)
        value = OMEGA * (update[:, :cases] + update[:, cases:])
        if before is not None:
            value = before[at, :] + value
        disp[at, :] = value
        high, low = split(value)
        pair[at, :cases] = high
        pair[at, cases:] = low
    for k in range(SLOTS):
        at = slice(k * rows, (k + 1) * rows)
        applied = jnp.dot(s_high[at, :], pair[...], preferred_element_type=F32)
        applied += jnp.dot(s_low[at, :], pair[...], preferred_element_type=F32)
        value = loads[at, :] - (applied[:, :cases] + applied[:, cases:])
        part[at, :] = jnp.where(row_mask(rows, sizes[k], cases), value, 0.0)
    for n, (slot, there) in enumerate(slots):
        outs[n][...] = part[slot_rows(slot, rows), :]


def final_kernel(mesh, roles, dirs, part, *rest):
    got, out = rest[: len(roles)], rest[len(roles)]
    rows = got[0].shape[0]
    out[...] = part[...]
    for n, role in enumerate(roles):
        slot, there = role_slot(mesh, dirs, role)
        at = slot_rows(slot, rows)
        out[at, :] = out[at, :] + jnp.where(there, 1.0, 0.0) * got[n][...]


def params(mib, **kw):
    return pltpu.CompilerParams(vmem_limit_bytes=mib << 20, **kw)


def shape(*dims, dtype=F32):
    return jax.ShapeDtypeStruct(dims, dtype)


def local(mesh, schur, loads, face_sizes, face_dir):
    matrix = schur[0, 0]
    load = loads[0, 0]
    sizes = face_sizes[0, 0]
    dirs = face_dir[0, 0]
    order, cases = load.shape
    rows = order // SLOTS
    roles = role_list(mesh)
    many = len(roles)

    sends = pl.pallas_call(
        functools.partial(pack_kernel, mesh, roles),
        name="pack",
        out_shape=[shape(rows, rows + cases)] * many,
        in_specs=[SMEM, SMEM, HBM, HBM],
        out_specs=[VMEM] * many,
        scratch_shapes=[pltpu.VMEM((many, rows, rows), F32), pltpu.VMEM((many, rows, cases), F32), pltpu.SemaphoreType.DMA((many, 2))],
        compiler_params=params(8),
    )(dirs, sizes, matrix, load)
    got = [exchange(mesh, role, value) for role, value in zip(roles, sends)]

    chunk = rows // 2
    s_high, s_low, diagonal = pl.pallas_call(
        split_kernel,
        name="split",
        out_shape=[shape(order, order, dtype=BF16), shape(order, order, dtype=BF16), shape(SLOTS, rows, rows)],
        in_specs=[HBM],
        out_specs=[VMEM] * 3,
        scratch_shapes=[pltpu.VMEM((2, chunk, order), F32), pltpu.SemaphoreType.DMA((2,))],
        compiler_params=params(20),
        cost_estimate=pl.CostEstimate(flops=4 * order * order, bytes_accessed=4 * order * order, transcendentals=0),
    )(matrix)

    i_high, i_low = pl.pallas_call(
        functools.partial(inverse_kernel, mesh, roles),
        name="inverse",
        out_shape=[shape(SLOTS, rows, rows, dtype=BF16)] * 2,
        in_specs=[SMEM, SMEM, VMEM] + [VMEM] * many,
        out_specs=[VMEM] * 2,
        scratch_shapes=[pltpu.VMEM((SLOTS, rows, rows), F32)],
        compiler_params=params(16),
    )(dirs, sizes, diagonal, *got)

    disp = part = None
    for step in range(ITERS):
        first = step == 0
        args = [dirs, sizes, s_high, s_low, i_high, i_low, load, *got] + ([] if first else [disp, part])
        disp, part, *sends = pl.pallas_call(
            functools.partial(step_kernel, mesh, roles, first),
            name=f"step{step}",
            out_shape=[shape(order, cases)] * 2 + [shape(rows, cases)] * many,
            in_specs=[SMEM, SMEM] + [VMEM] * (len(args) - 2),
            out_specs=[VMEM] * (2 + many),
            scratch_shapes=[pltpu.VMEM((order, cases), F32), pltpu.VMEM((order, 2 * cases), BF16)],
            compiler_params=params(24),
        )(*args)
        got = [exchange(mesh, role, value) for role, value in zip(roles, sends)]

    final = pl.pallas_call(
        functools.partial(final_kernel, mesh, roles),
        name="final",
        out_shape=shape(order, cases),
        in_specs=[SMEM] + [VMEM] * (1 + many),
        out_specs=VMEM,
        compiler_params=params(8),
    )(dirs, part, *got)
    return disp[None, None], final[None, None]


def solution(mesh):
    return jax.shard_map(
        functools.partial(local, mesh),
        mesh=mesh,
        in_specs=(
            P("wide", "depth", None, None),
            P("wide", "depth", None, None),
            P("wide", "depth", None),
            P("wide", "depth", None),
        ),
        out_specs=(P("wide", "depth", None, None), P("wide", "depth", None, None)),
        check_vma=False,
    )
```

time: 514 us -> 70.4 us (0.14)
  the two profiles are of different devices: /device:TPU:8 before, /device:TPU:0 now
where the time goes in v1:
time: 70.4 us; the launch traced here: 70.1 us
  Pallas kernels  35.4 us (50%)
  starting transfers between devices  16.5 us (23%)
  waiting for transfers between devices  11.4 us (16%)
  local copies, waits for them, and re-layouts  6.13 us (9%)
  between operations  0.71 us (1%)
    pallas_call x1, Pallas kernels, local(): pl.pallas_call(functools.partial(inverse_kernel, mesh, roles), name='inve...  22.4 us
    ppermute x9, starting transfers between devices, exchange(): return lax.ppermute(value, ('wide', 'depth'), sorted(perm))  16.5 us
    ppermute x9, waiting for transfers between devices, exchange(): return lax.ppermute(value, ('wide', 'depth'), sorted(perm))  11.4 us
    pallas_call x2, Pallas kernels, local(): pl.pallas_call(functools.partial(step_kernel, mesh, roles, first), name=f...  8.19 us
    unnamed x16, local copies, waits for them, and re-layouts  6.13 us
    pallas_call x1, Pallas kernels, local(): pl.pallas_call(split_kernel, name='split', out_shape=[shape(order, order,...  2.01 us
    pallas_call x1, Pallas kernels, local(): pl.pallas_call(functools.partial(final_kernel, mesh, roles), name='final'...  1.52 us
  transfers between devices with their start and end apart: 9, of which 5 were waited for; matrix products, arithmetic and copies ran while one was open for 0% of the time, Pallas kernels for 3%

profile of v1, /device:TPU:0, one launch (start us, length us, event | category | flops | bytes accessed | tf_op | source)
XLA Modules:
  0.0 70.1 jit_solution(7646797562459602335)
XLA Ops:
  0.6 0.0 copy-start
  0.6 3.7 %copy-done = f32[1,1,1536,1536]{3,2,1,0:T(8,128)S(1)} copy-done((f32[1,1,1536,1536]{3,2,1,0:T(8,128)S(1)}, f32[1,1,1536,1536]{3,2,1,0:T(8,128)}, u32[]{:S(2)}) %copy-start) | copy-done | bytes 9437208
  4.3 0.0 copy-start.2
  4.3 1.1 %copy-done.2 = f32[1,1,1536,128]{3,2,1,0:T(8,128)S(1)} copy-done((f32[1,1,1536,128]{3,2,1,0:T(8,128)S(1)}, f32[1,1,1536,128]{3,2,1,0:T(8,128)}, u32[]{:S(2)}) %copy-start.2) | copy-done | bytes 786456
  5.4 0.0 copy-start.4
  5.4 0.7 copy-done.4
  6.1 0.0 copy-start.6
  6.1 0.7 copy-done.6
  6.8 0.0 copy-start.1
  6.8 1.3 %pack.1 = (f32[256,384]{1,0:T(8,128)S(1)}, f32[256,384]{1,0:T(8,128)S(1)}, f32[256,384]{1,0:T(8,128)S(1)}) custom-call(s32[6]{0:T(128)S(1)} %bitcast.11, s32[6]{0:T(128)S(1)} %bitcast.16, f32[1536,1536]{1,0:T(8,128)S(1)} %bitcast.6, f32[1536,128]{1,0:T(8,128)S(1)} %bitcast.8), custom_call_target="tpu_custom_call" | custom-call | tf_op jit(solution)/shard_map/pack/pallas_call | solution.py:315
  8.1 0.6 collective-permute-start
  8.6 5.6 %collective-permute-start.1 = (f32[256,384]{1,0:T(8,128)S(1)}, f32[256,384]{1,0:T(8,128)S(1)}, u32[]{:S(2)}, u32[]{:S(2)}) collective-permute-start(f32[256,384]{1,0:T(8,128)S(1)} %get-tuple-element.24), channel_id=1, source_target_pairs={{0,30},{1,31},{2,4},{3,5},{4,2},{5,3},{6,8},{7,9},{8,6},{9,7},{10,... | collective-permute-start | bytes 1179656 | tf_op jit(solution)/shard_map/ppermute | solution.py:62
  14.3 0.0 copy-start.5
  14.3 0.0 copy-start.7
  14.3 0.0 copy-start.3
  14.3 1.5 %collective-permute-start.2 = (f32[256,384]{1,0:T(8,128)S(1)}, f32[256,384]{1,0:T(8,128)S(1)}, u32[]{:S(2)}, u32[]{:S(2)}) collective-permute-start(f32[256,384]{1,0:T(8,128)S(1)} %get-tuple-element.25), channel_id=1, source_target_pairs={{0,1},{1,0},{2,3},{3,2},{4,5},{5,4},{6,7},{7,6},{8,9},{9,8},{10,11... | collective-permute-start | bytes 1179656 | tf_op jit(solution)/shard_map/ppermute | solution.py:62
  15.8 0.0 copy-done.1
  15.8 2.0 %split.1 = (bf16[1536,1536]{1,0:T(8,128)(2,1)S(1)}, bf16[1536,1536]{1,0:T(8,128)(2,1)S(1)}, f32[6,256,256]{2,1,0:T(8,128)S(1)}) custom-call(f32[1536,1536]{1,0:T(8,128)S(1)} %bitcast.7), custom_call_target="tpu_custom_call" | custom-call | flops 9437184 | bytes 9437184 | tf_op jit(solution)/shard_map/split/pallas_call | solution.py:327
  17.8 0.0 collective-permute-done.rest_0_
  17.8 2.0 %collective-permute-done.1.rest_1_ = f32[256,384]{1,0:T(8,128)S(1)} collective-permute-done((f32[256,384]{1,0:T(8,128)S(1)}, f32[256,384]{1,0:T(8,128)S(1)}, u32[]{:S(2)}, u32[]{:S(2)}) %collective-permute-start.1) | collective-permute-done | bytes 393248 | tf_op jit(solution)/shard_map/ppermute | solution.py:62
  19.8 2.5 %collective-permute-done.2.rest_2_ = f32[256,384]{1,0:T(8,128)S(1)} collective-permute-done((f32[256,384]{1,0:T(8,128)S(1)}, f32[256,384]{1,0:T(8,128)S(1)}, u32[]{:S(2)}, u32[]{:S(2)}) %collective-permute-start.2) | collective-permute-done | bytes 393248 | tf_op jit(solution)/shard_map/ppermute | solution.py:62
  22.3 0.0 copy-done.5
  22.3 0.0 copy-done.7
  22.3 22.4 %inverse.1 = (bf16[6,256,256]{2,1,0:T(8,128)(2,1)S(1)}, bf16[6,256,256]{2,1,0:T(8,128)(2,1)S(1)}) custom-call(s32[6]{0:T(128)S(1)} %bitcast.12, s32[6]{0:T(128)S(1)} %bitcast.17, f32[6,256,256]{2,1,0:T(8,128)S(1)} %get-tuple-element.22.diagonal, f32[256,384]{1,0:T(8,128)S(1)} %collective-permute-done.rest_0_, f32[256,384]{1,0:T(8,128)S(1)} %collective-permute-done.1.rest_1_, ...), custom_call_target="tpu_custom_call" | custom-call | tf_op jit(solution)/shard_map/inverse/pallas_call | solution.py:338
  44.7 0.0 copy-done.3
  44.8 3.8 %step0.1 = (f32[1536,128]{1,0:T(8,128)S(1)}, f32[1536,128]{1,0:T(8,128)S(1)}, f32[256,128]{1,0:T(8,128)S(1)}, f32[256,128]{1,0:T(8,128)S(1)}, f32[256,128]{1,0:T(8,128)S(1)}) custom-call(s32[6]{0:T(128)S(1)} %bitcast.13, s32[6]{0:T(128)S(1)} %bitcast.18, bf16[1536,1536]{1,0:T(8,128)(2,1)S(1)} %get-tuple-element.20.s_high, ...), custom_call_target="tpu_custom_call" | custom-call | tf_op jit(solution)/shard_map/step0/pallas_call | solution.py:352
  48.5 0.1 collective-permute-start.3
  48.6 3.5 %collective-permute-start.4 = (f32[256,128]{1,0:T(8,128)S(1)}, f32[256,128]{1,0:T(8,128)S(1)}, u32[]{:S(2)}, u32[]{:S(2)}) collective-permute-start(f32[256,128]{1,0:T(8,128)S(1)} %get-tuple-element.29), channel_id=1, source_target_pairs={{0,30},{1,31},{2,4},{3,5},{4,2},{5,3},{6,8},{7,9},{8,6},{9,7},{10,... | collective-permute-start | bytes 393224 | tf_op jit(solution)/shard_map/ppermute | solution.py:62
  52.1 1.5 %collective-permute-start.5 = (f32[256,128]{1,0:T(8,128)S(1)}, f32[256,128]{1,0:T(8,128)S(1)}, u32[]{:S(2)}, u32[]{:S(2)}) collective-permute-start(f32[256,128]{1,0:T(8,128)S(1)} %get-tuple-element.30), channel_id=1, source_target_pairs={{0,1},{1,0},{2,3},{3,2},{4,5},{5,4},{6,7},{7,6},{8,9},{9,8},{10,11... | collective-permute-start | bytes 393224 | tf_op jit(solution)/shard_map/ppermute | solution.py:62
  53.7 0.0 collective-permute-done.3.rest_0_
  53.7 2.1 %collective-permute-done.4.rest_1_ = f32[256,128]{1,0:T(8,128)S(1)} collective-permute-done((f32[256,128]{1,0:T(8,128)S(1)}, f32[256,128]{1,0:T(8,128)S(1)}, u32[]{:S(2)}, u32[]{:S(2)}) %collective-permute-start.4) | collective-permute-done | bytes 131104 | tf_op jit(solution)/shard_map/ppermute | solution.py:62
  55.8 1.3 %collective-permute-done.5.rest_2_ = f32[256,128]{1,0:T(8,128)S(1)} collective-permute-done((f32[256,128]{1,0:T(8,128)S(1)}, f32[256,128]{1,0:T(8,128)S(1)}, u32[]{:S(2)}, u32[]{:S(2)}) %collective-permute-start.5) | collective-permute-done | bytes 131104 | tf_op jit(solution)/shard_map/ppermute | solution.py:62
  57.1 4.4 %step1.1 = (f32[1536,128]{1,0:T(8,128)}, f32[1536,128]{1,0:T(8,128)S(1)}, f32[256,128]{1,0:T(8,128)S(1)}, f32[256,128]{1,0:T(8,128)S(1)}, f32[256,128]{1,0:T(8,128)S(1)}) custom-call(s32[6]{0:T(128)S(1)} %bitcast.14, s32[6]{0:T(128)S(1)} %bitcast.19, bf16[1536,1536]{1,0:T(8,128)(2,1)S(1)} %get-tuple-element.20.s_high, ...), custom_call_target="tpu_custom_call" | custom-call | tf_op jit(solution)/shard_map/step1/pallas_call | solution.py:352
  61.5 0.0 collective-permute-start.6
  61.5 2.1 %collective-permute-start.7 = (f32[256,128]{1,0:T(8,128)S(1)}, f32[256,128]{1,0:T(8,128)S(1)}, u32[]{:S(2)}, u32[]{:S(2)}) collective-permute-start(f32[256,128]{1,0:T(8,128)S(1)} %get-tuple-element.36), channel_id=1, source_target_pairs={{0,30},{1,31},{2,4},{3,5},{4,2},{5,3},{6,8},{7,9},{8,6},{9,7},{10,... | collective-permute-start | bytes 393224 | tf_op jit(solution)/shard_map/ppermute | solution.py:62
  63.7 1.5 %collective-permute-start.8 = (f32[256,128]{1,0:T(8,128)S(1)}, f32[256,128]{1,0:T(8,128)S(1)}, u32[]{:S(2)}, u32[]{:S(2)}) collective-permute-start(f32[256,128]{1,0:T(8,128)S(1)} %get-tuple-element.37), channel_id=1, source_target_pairs={{0,1},{1,0},{2,3},{3,2},{4,5},{5,4},{6,7},{7,6},{8,9},{9,8},{10,11... | collective-permute-start | bytes 393224 | tf_op jit(solution)/shard_map/ppermute | solution.py:62
  65.2 0.0 collective-permute-done.6.rest_0_
  65.2 3.4 %collective-permute-done.7.rest_1_ = f32[256,128]{1,0:T(8,128)S(1)} collective-permute-done((f32[256,128]{1,0:T(8,128)S(1)}, f32[256,128]{1,0:T(8,128)S(1)}, u32[]{:S(2)}, u32[]{:S(2)}) %collective-permute-start.7) | collective-permute-done | bytes 131104 | tf_op jit(solution)/shard_map/ppermute | solution.py:62
  68.6 0.0 collective-permute-done.8.rest_2_
  68.6 1.5 %final.1 = f32[1536,128]{1,0:T(8,128)} custom-call(s32[6]{0:T(128)S(1)} %bitcast.15, f32[1536,128]{1,0:T(8,128)S(1)} %get-tuple-element.34.part, f32[256,128]{1,0:T(8,128)S(1)} %collective-permute-done.6.rest_0_, f32[256,128]{1,0:T(8,128)S(1)} %collective-permute-done.7.rest_1_, f32[256,128]{1,0:T(8,128)S(1)} %collective-permute-done.8.rest_2_), custom_call_target="tpu_custom_call" | custom-call | tf_op jit(solution)/shard_map/final/pallas_call | solution.py:363
Async XLA Ops:
  0.6 3.7 %copy-start = (f32[1,1,1536,1536]{3,2,1,0:T(8,128)S(1)}, f32[1,1,1536,1536]{3,2,1,0:T(8,128)}, u32[]{:S(2)}) copy-start(f32[1,1,1536,1536]{3,2,1,0:T(8,128)} %param.4) | copy-start | bytes 28311556
  4.3 1.1 %copy-start.2 = (f32[1,1,1536,128]{3,2,1,0:T(8,128)S(1)}, f32[1,1,1536,128]{3,2,1,0:T(8,128)}, u32[]{:S(2)}) copy-start(f32[1,1,1536,128]{3,2,1,0:T(8,128)} %param.5) | copy-start | bytes 2359300
  5.4 0.7 copy-start.4
  6.1 0.7 copy-start.6
  6.8 9.0 %copy-start.1 = (f32[1,1,1536,1536]{3,2,1,0:T(8,128)S(1)}, f32[1,1,1536,1536]{3,2,1,0:T(8,128)}, u32[]{:S(2)}) copy-start(f32[1,1,1536,1536]{3,2,1,0:T(8,128)} %param.4) | copy-start | bytes 28311556
  8.1 9.7 %collective-permute-start = (f32[256,384]{1,0:T(8,128)S(1)}, f32[256,384]{1,0:T(8,128)S(1)}, u32[]{:S(2)}, u32[]{:S(2)}) collective-permute-start(f32[256,384]{1,0:T(8,128)S(1)} %get-tuple-element.23), channel_id=1, source_target_pairs={{0,2},{1,3},{2,0},{3,1},{4,6},{5,7},{6,4},{7,5},{8,10},{9,11},{10,... | collective-permute-start | bytes 1179656 | tf_op jit(solution)/shard_map/ppermute | solution.py:62
  8.6 11.2 %collective-permute-start.1 = (f32[256,384]{1,0:T(8,128)S(1)}, f32[256,384]{1,0:T(8,128)S(1)}, u32[]{:S(2)}, u32[]{:S(2)}) collective-permute-start(f32[256,384]{1,0:T(8,128)S(1)} %get-tuple-element.24), channel_id=1, source_target_pairs={{0,30},{1,31},{2,4},{3,5},{4,2},{5,3},{6,8},{7,9},{8,6},{9,7},{10,... | collective-permute-start | bytes 1179656 | tf_op jit(solution)/shard_map/ppermute | solution.py:62
  14.3 8.1 %copy-start.5 = (s32[1,1,6]{2,1,0:T(1,128)S(1)}, s32[1,1,6]{2,1,0:T(1,128)}, u32[]{:S(2)}) copy-start(s32[1,1,6]{2,1,0:T(1,128)} %param.7) | copy-start | bytes 76
  14.3 8.1 %copy-start.7 = (s32[1,1,6]{2,1,0:T(1,128)S(1)}, s32[1,1,6]{2,1,0:T(1,128)}, u32[]{:S(2)}) copy-start(s32[1,1,6]{2,1,0:T(1,128)} %param.6) | copy-start | bytes 76
  14.3 30.5 %copy-start.3 = (f32[1,1,1536,128]{3,2,1,0:T(8,128)S(1)}, f32[1,1,1536,128]{3,2,1,0:T(8,128)}, u32[]{:S(2)}) copy-start(f32[1,1,1536,128]{3,2,1,0:T(8,128)} %param.5) | copy-start | bytes 2359300
  14.3 8.1 %collective-permute-start.2 = (f32[256,384]{1,0:T(8,128)S(1)}, f32[256,384]{1,0:T(8,128)S(1)}, u32[]{:S(2)}, u32[]{:S(2)}) collective-permute-start(f32[256,384]{1,0:T(8,128)S(1)} %get-tuple-element.25), channel_id=1, source_target_pairs={{0,1},{1,0},{2,3},{3,2},{4,5},{5,4},{6,7},{7,6},{8,9},{9,8},{10,11... | collective-permute-start | bytes 1179656 | tf_op jit(solution)/shard_map/ppermute | solution.py:62
  48.5 5.1 %collective-permute-start.3 = (f32[256,128]{1,0:T(8,128)S(1)}, f32[256,128]{1,0:T(8,128)S(1)}, u32[]{:S(2)}, u32[]{:S(2)}) collective-permute-start(f32[256,128]{1,0:T(8,128)S(1)} %get-tuple-element.28), channel_id=1, source_target_pairs={{0,2},{1,3},{2,0},{3,1},{4,6},{5,7},{6,4},{7,5},{8,10},{9,11},{10,... | collective-permute-start | bytes 393224 | tf_op jit(solution)/shard_map/ppermute | solution.py:62
  48.6 7.2 %collective-permute-start.4 = (f32[256,128]{1,0:T(8,128)S(1)}, f32[256,128]{1,0:T(8,128)S(1)}, u32[]{:S(2)}, u32[]{:S(2)}) collective-permute-start(f32[256,128]{1,0:T(8,128)S(1)} %get-tuple-element.29), channel_id=1, source_target_pairs={{0,30},{1,31},{2,4},{3,5},{4,2},{5,3},{6,8},{7,9},{8,6},{9,7},{10,... | collective-permute-start | bytes 393224 | tf_op jit(solution)/shard_map/ppermute | solution.py:62
  52.1 5.0 %collective-permute-start.5 = (f32[256,128]{1,0:T(8,128)S(1)}, f32[256,128]{1,0:T(8,128)S(1)}, u32[]{:S(2)}, u32[]{:S(2)}) collective-permute-start(f32[256,128]{1,0:T(8,128)S(1)} %get-tuple-element.30), channel_id=1, source_target_pairs={{0,1},{1,0},{2,3},{3,2},{4,5},{5,4},{6,7},{7,6},{8,9},{9,8},{10,11... | collective-permute-start | bytes 393224 | tf_op jit(solution)/shard_map/ppermute | solution.py:62
  61.5 3.7 %collective-permute-start.6 = (f32[256,128]{1,0:T(8,128)S(1)}, f32[256,128]{1,0:T(8,128)S(1)}, u32[]{:S(2)}, u32[]{:S(2)}) collective-permute-start(f32[256,128]{1,0:T(8,128)S(1)} %get-tuple-element.35), channel_id=1, source_target_pairs={{0,2},{1,3},{2,0},{3,1},{4,6},{5,7},{6,4},{7,5},{8,10},{9,11},{10,... | collective-permute-start | bytes 393224 | tf_op jit(solution)/shard_map/ppermute | solution.py:62
  61.5 7.1 %collective-permute-start.7 = (f32[256,128]{1,0:T(8,128)S(1)}, f32[256,128]{1,0:T(8,128)S(1)}, u32[]{:S(2)}, u32[]{:S(2)}) collective-permute-start(f32[256,128]{1,0:T(8,128)S(1)} %get-tuple-element.36), channel_id=1, source_target_pairs={{0,30},{1,31},{2,4},{3,5},{4,2},{5,3},{6,8},{7,9},{8,6},{9,7},{10,... | collective-permute-start | bytes 393224 | tf_op jit(solution)/shard_map/ppermute | solution.py:62
  63.7 5.0 %collective-permute-start.8 = (f32[256,128]{1,0:T(8,128)S(1)}, f32[256,128]{1,0:T(8,128)S(1)}, u32[]{:S(2)}, u32[]{:S(2)}) collective-permute-start(f32[256,128]{1,0:T(8,128)S(1)} %get-tuple-element.37), channel_id=1, source_target_pairs={{0,1},{1,0},{2,3},{3,2},{4,5},{5,4},{6,7},{7,6},{8,9},{9,8},{10,11... | collective-permute-start | bytes 393224 | tf_op jit(solution)/shard_map/ppermute | solution.py:62

commit v2 on v1

--- a/solution.py
+++ b/solution.py
@@ -12,7 +12,7 @@
 
 SLOTS = 6
 LANES = 128
-OUTER = 64
+OUTER = 32
 MICRO = 8
 F32 = jnp.float32
 BF16 = jnp.bfloat16
@@ -76,7 +76,7 @@
     rows, packs = len(d), len(d[0])
     lane = lax.broadcasted_iota(jnp.int32, (MICRO, LANES), 1)
     sub = lax.broadcasted_iota(jnp.int32, (MICRO, LANES), 0)
-    half = lane & OUTER
+    half = lane - (lane & (OUTER - 1))
     local = lane & (OUTER - 1)
     for q in range(rows):
         own = (local >= q * MICRO) & (local < (q + 1) * MICRO)
@@ -115,62 +115,104 @@
     return high, (x - high.astype(F32)).astype(BF16)
 
 
+def left(x):
+    return jnp.concatenate(split(x), 1)
+
+
+def right(x):
+    high, low = split(x)
+    return jnp.concatenate([jnp.concatenate([high, low], 1), jnp.concatenate([high, jnp.zeros_like(low)], 1)], 0)
+
+
+def product(one, two):
+    both = jnp.dot(one, two, preferred_element_type=F32)
+    half = both.shape[1] // 2
+    return both[:, :half] + both[:, half:]
+
+
+def lane_group(rows):
+    return lax.broadcasted_iota(jnp.int32, (rows, LANES), 1) // OUTER
+
+
+def packed(a_ref, rows, cl, s, fill=0.0):
+    groups = LANES // OUTER
+    height = rows.stop - rows.start
+    group = lane_group(height)
+    out = []
+    for first in range(0, a_ref.shape[0], groups):
+        pack = None
+        for g in range(first, min(a_ref.shape[0], first + groups)):
+            to = g - first
+            x = a_ref[g, rows, cl]
+            if to != s:
+                x = pltpu.roll(x, ((to - s) * OUTER) % LANES, 1)
+            pack = x if pack is None else jnp.where(group >= to, x, pack)
+        if to + 1 < groups:
+            spare = jnp.zeros_like(pack)
+            if fill:
+                spare = jnp.where(lax.broadcasted_iota(jnp.int32, pack.shape, 1) % OUTER == lax.broadcasted_iota(jnp.int32, pack.shape, 0), fill, spare)
+            pack = jnp.where(group > to, spare, pack)
+        out.append(pack)
+    return out
+
+
+def block_diagonal(x):
+    group = lane_group(OUTER)
+    return jnp.concatenate([jnp.where(group == k, x, 0.0) for k in range(LANES // OUTER)], 0)
+
+
+def invert_tile(a_ref, rl, cl):
+    count = a_ref.shape[0]
+    groups = LANES // OUTER
+    pieces = OUTER // MICRO
+    bands = [slice(rl.start + s * OUTER, rl.start + (s + 1) * OUTER) for s in range(groups)]
+    group_row, group_all = lane_group(OUTER), lane_group(LANES)
+    d = packed(a_ref, bands[0], cl, 0, 1.0)
+    for s in range(groups):
+        lines = [[x[i * MICRO : (i + 1) * MICRO] for x in d] for i in range(pieces)]
+        lines = invert_diagonal(lines)
+        packs = [jnp.concatenate([lines[i][p] for i in range(pieces)], 0) for p in range(len(d))]
+        if s + 1 < groups:
+            ahead = packed(a_ref, bands[s], cl, s + 1)
+            below = packed(a_ref, bands[s + 1], cl, s)
+            d = packed(a_ref, bands[s + 1], cl, s + 1, 1.0)
+            for p, w in enumerate(packs):
+                row = product(left(w), right(block_diagonal(ahead[p])))
+                d[p] = d[p] - product(left(below[p]), right(block_diagonal(row)))
+        for g in range(count):
+            p, at = divmod(g, groups)
+            w = packs[p]
+            if at != s:
+                w = pltpu.roll(w, ((s - at) * OUTER) % LANES, 1)
+            w = jnp.where(group_row == s, w, 0.0)
+            t = a_ref[g, rl, cl]
+            row = jnp.where(group_row == s, w, product(left(w), right(t)))
+            parts = [jnp.zeros((OUTER, LANES), F32)] * groups
+            parts[s] = row
+            change = product(left(t), right(jnp.concatenate(parts, 0)))
+            a_ref[g, rl, cl] = jnp.where(group_all == s, 0.0, t) - change
+            a_ref[g, bands[s], cl] = row
+
+
 def invert_blocks(a_ref):
     count, size = a_ref.shape[0], a_ref.shape[-1]
-    lane = lax.broadcasted_iota(jnp.int32, (MICRO, LANES), 1)
-    for block in range(size // OUTER):
-        r0 = block * OUTER
-        tile, h = divmod(r0, LANES)
-        h //= OUTER
-        tl = slice(tile * LANES, (tile + 1) * LANES)
-        d = []
-        for i in range(OUTER // MICRO):
-            rows = slice(r0 + i * MICRO, r0 + (i + 1) * MICRO)
-            line = []
-            for p in range(count // 2):
-                x, y = a_ref[2 * p, rows, tl], a_ref[2 * p + 1, rows, tl]
-                if h == 0:
-                    line.append(jnp.where(lane < OUTER, x, pltpu.roll(y, OUTER, 1)))
-                else:
-                    line.append(jnp.where(lane < OUTER, pltpu.roll(x, OUTER, 1), y))
-            d.append(line)
-        d = invert_diagonal(d)
-        lane_row = lax.broadcasted_iota(jnp.int32, (OUTER, LANES), 1)
-        own_row = (lane_row >= OUTER * h) & (lane_row < OUTER * (h + 1))
-        lane_all = lax.broadcasted_iota(jnp.int32, (size, LANES), 1)
-        own_all = (lane_all >= OUTER * h) & (lane_all < OUTER * (h + 1))
+    tiles = [slice(b * LANES, (b + 1) * LANES) for b in range(size // LANES)]
+    for own in tiles:
+        invert_tile(a_ref, own, own)
+        others = [t for t in tiles if t is not own]
         for g in range(count):
-            p, s = divmod(g, 2)
-            w = jnp.concatenate([d[i][p] for i in range(OUTER // MICRO)], 0)
-            if s != h:
-                w = pltpu.roll(w, OUTER, 1)
-            w = jnp.where(own_row, w, 0.0)
-            w_high = w.astype(BF16)
-            w_mixed = (w + pltpu.roll(w - w_high.astype(F32), OUTER, 1)).astype(BF16)
-            high, low = split(a_ref[g, r0 : r0 + OUTER, :])
-            zero = jnp.zeros_like(low)
-            right = jnp.concatenate([high, high, low, zero] if h == 0 else [high, high, zero, low], 0)
-            row = jnp.dot(jnp.concatenate([w_mixed, w_high], 1), right, preferred_element_type=F32)
-            row = jnp.concatenate(
-                [
-                    jnp.where(own_row, w, row[:, c * LANES : (c + 1) * LANES]) if c == tile else row[:, c * LANES : (c + 1) * LANES]
-                    for c in range(size // LANES)
-                ],
-                1,
-            )
-            column = a_ref[g, :, tl]
-            c_high = column.astype(BF16)
-            c_mixed = jnp.where(own_all, column, pltpu.roll(column - c_high.astype(F32), OUTER, 1)).astype(BF16)
-            high, low = split(row)
-            right = jnp.concatenate([high, high, low, zero] if h == 0 else [high, high, zero, low], 0)
-            change = jnp.dot(jnp.concatenate([c_mixed, c_high], 1), right, preferred_element_type=F32)
-            for c in range(size // LANES):
-                cl = slice(c * LANES, (c + 1) * LANES)
-                base = a_ref[g, :, cl]
-                if c == tile:
-                    base = jnp.where(own_all, 0.0, base)
-                a_ref[g, :, cl] = base - change[:, cl]
-            a_ref[g, r0 : r0 + OUTER, :] = row
+            x = a_ref[g, own, own]
+            x_left, x_right = left(x), right(x)
+            columns = [left(a_ref[g, t, own]) for t in others]
+            rows = []
+            for t in others:
+                row = product(x_left, right(a_ref[g, own, t]))
+                a_ref[g, own, t] = row
+                rows.append(right(row))
+            for i, ti in enumerate(others):
+                for j, tj in enumerate(others):
+                    a_ref[g, ti, tj] = a_ref[g, ti, tj] - product(columns[i], rows[j])
+                a_ref[g, ti, own] = -product(columns[i], x_right)
 
 
 def slot_rows(slot, rows):
@@ -319,7 +361,7 @@
         in_specs=[SMEM, SMEM, HBM, HBM],
         out_specs=[VMEM] * many,
         scratch_shapes=[pltpu.VMEM((many, rows, rows), F32), pltpu.VMEM((many, rows, cases), F32), pltpu.SemaphoreType.DMA((many, 2))],
-        compiler_params=params(8),
+        compiler_params=params(60),
     )(dirs, sizes, matrix, load)
     got = [exchange(mesh, role, value) for role, value in zip(roles, sends)]
 
@@ -331,7 +373,7 @@
         in_specs=[HBM],
         out_specs=[VMEM] * 3,
         scratch_shapes=[pltpu.VMEM((2, chunk, order), F32), pltpu.SemaphoreType.DMA((2,))],
-        compiler_params=params(20),
+        compiler_params=params(40),
         cost_estimate=pl.CostEstimate(flops=4 * order * order, bytes_accessed=4 * order * order, transcendentals=0),
     )(matrix)
 

time: 70.4 us -> 60.8 us (0.86)
  local copies, waits for them, and re-layouts: 6.13 us -> 0.01 us
  waiting for transfers between devices: 11.4 us -> 7.79 us
  Pallas kernels: 35.4 us -> 36.6 us
  starting transfers between devices: 16.5 us -> 15.4 us
    pallas_call x1, Pallas kernels: 22.4 us -> 16.1 us  [local(): pl.pallas_call(functools.partial(inverse_kernel, mesh, roles), name='inve...]
    unnamed x16 -> x6, local copies, waits for them, and re-layouts: 6.13 us -> 0.01 us
    pallas_call x1, Pallas kernels: 2.01 us -> 7.79 us  [local(): pl.pallas_call(split_kernel, name='split', out_shape=[shape(order, order,...]
    ppermute x9, waiting for transfers between devices: 11.4 us -> 7.79 us  [exchange(): return lax.ppermute(value, ('wide', 'depth'), sorted(perm))]
    pallas_call x1, Pallas kernels: 1.3 us -> 3.02 us  [local(): pl.pallas_call(functools.partial(pack_kernel, mesh, roles), name='pack',...]
    ppermute x9, starting transfers between devices: 16.5 us -> 15.4 us  [exchange(): return lax.ppermute(value, ('wide', 'depth'), sorted(perm))]
  transfers between devices with their start and end apart: 9 -> 9, of which waited for: 5 -> 4; matrix products, arithmetic and copies ran while one was open for 0% -> 0% of each run, Pallas kernels for 3% -> 13%
where the time goes in v2:
time: 60.8 us; the launch traced here: 60.5 us
  Pallas kernels  36.6 us (60%)
  starting transfers between devices  15.4 us (25%)
  waiting for transfers between devices  7.79 us (13%)
  between operations  0.72 us (1%)
    pallas_call x1, Pallas kernels, local(): pl.pallas_call(functools.partial(inverse_kernel, mesh, roles), name='inve...  16.1 us
    ppermute x9, starting transfers between devices, exchange(): return lax.ppermute(value, ('wide', 'depth'), sorted(perm))  15.4 us
    pallas_call x2, Pallas kernels, local(): pl.pallas_call(functools.partial(step_kernel, mesh, roles, first), name=f...  8.18 us
    ppermute x9, waiting for transfers between devices, exchange(): return lax.ppermute(value, ('wide', 'depth'), sorted(perm))  7.79 us
    pallas_call x1, Pallas kernels, local(): pl.pallas_call(split_kernel, name='split', out_shape=[shape(order, order,...  7.79 us
    pallas_call x1, Pallas kernels, local(): pl.pallas_call(functools.partial(pack_kernel, mesh, roles), name='pack',...  3.02 us
    pallas_call x1, Pallas kernels, local(): pl.pallas_call(functools.partial(final_kernel, mesh, roles), name='final'...  1.52 us
  transfers between devices with their start and end apart: 9, of which 4 were waited for; matrix products, arithmetic and copies ran while one was open for 0% of the time, Pallas kernels for 13%

profile of v2, /device:TPU:0, one launch (start us, length us, event | category | flops | bytes accessed | tf_op | source)
XLA Modules:
  0.0 60.5 jit_solution(11576835634710444377)
XLA Ops:
  0.6 3.0 %pack.1 = (f32[256,384]{1,0:T(8,128)}, f32[256,384]{1,0:T(8,128)}, f32[256,384]{1,0:T(8,128)}) custom-call(s32[6]{0:T(128)} %bitcast.9, s32[6]{0:T(128)} %bitcast.14, f32[1536,1536]{1,0:T(8,128)} %bitcast.18, f32[1536,128]{1,0:T(8,128)} %bitcast.6), custom_call_target="tpu_custom_call" | custom-call | tf_op jit(solution)/shard_map/pack/pallas_call | solution.py:357
  3.7 0.6 collective-permute-start
  4.2 5.6 %collective-permute-start.1 = (f32[256,384]{1,0:T(8,128)}, f32[256,384]{1,0:T(8,128)S(1)}, u32[]{:S(2)}, u32[]{:S(2)}) collective-permute-start(f32[256,384]{1,0:T(8,128)} %get-tuple-element.24), channel_id=1, source_target_pairs={{0,30},{1,31},{2,4},{3,5},{4,2},{5,3},{6,8},{7,9},{8,6},{9,7},{10,... | collective-permute-start | bytes 1179656 | tf_op jit(solution)/shard_map/ppermute | solution.py:62
  9.8 0.0 copy-start.1
  9.8 0.0 copy-start.2
  9.8 0.0 copy-start
  9.8 1.5 %collective-permute-start.2 = (f32[256,384]{1,0:T(8,128)}, f32[256,384]{1,0:T(8,128)S(1)}, u32[]{:S(2)}, u32[]{:S(2)}) collective-permute-start(f32[256,384]{1,0:T(8,128)} %get-tuple-element.25), channel_id=1, source_target_pairs={{0,1},{1,0},{2,3},{3,2},{4,5},{5,4},{6,7},{7,6},{8,9},{9,8},{10,11... | collective-permute-start | bytes 1179656 | tf_op jit(solution)/shard_map/ppermute | solution.py:62
  11.4 7.8 %split.1 = (bf16[1536,1536]{1,0:T(8,128)(2,1)S(1)}, bf16[1536,1536]{1,0:T(8,128)(2,1)S(1)}, f32[6,256,256]{2,1,0:T(8,128)S(1)}) custom-call(f32[1536,1536]{1,0:T(8,128)} %bitcast.19), custom_call_target="tpu_custom_call" | custom-call | flops 9437184 | bytes 9437184 | tf_op jit(solution)/shard_map/split/pallas_call | solution.py:369
  19.2 0.0 collective-permute-done.rest_0_
  19.2 0.0 collective-permute-done.1.rest_1_
  19.2 0.0 collective-permute-done.2.rest_2_
  19.2 0.0 copy-done.1
  19.2 0.0 copy-done.2
  19.2 16.1 %inverse.1 = (bf16[6,256,256]{2,1,0:T(8,128)(2,1)S(1)}, bf16[6,256,256]{2,1,0:T(8,128)(2,1)S(1)}) custom-call(s32[6]{0:T(128)S(1)} %bitcast.10, s32[6]{0:T(128)S(1)} %bitcast.15, f32[6,256,256]{2,1,0:T(8,128)S(1)} %get-tuple-element.22.diagonal, f32[256,384]{1,0:T(8,128)S(1)} %collective-permute-done.rest_0_, f32[256,384]{1,0:T(8,128)S(1)} %collective-permute-done.1.rest_1_, ...), custom_call_target="tpu_custom_call" | custom-call | tf_op jit(solution)/shard_map/inverse/pallas_call | solution.py:380
  35.3 0.0 copy-done
  35.4 3.8 %step0.1 = (f32[1536,128]{1,0:T(8,128)S(1)}, f32[1536,128]{1,0:T(8,128)S(1)}, f32[256,128]{1,0:T(8,128)S(1)}, f32[256,128]{1,0:T(8,128)S(1)}, f32[256,128]{1,0:T(8,128)S(1)}) custom-call(s32[6]{0:T(128)S(1)} %bitcast.11, s32[6]{0:T(128)S(1)} %bitcast.16, bf16[1536,1536]{1,0:T(8,128)(2,1)S(1)} %get-tuple-element.20.s_high, ...), custom_call_target="tpu_custom_call" | custom-call | tf_op jit(solution)/shard_map/step0/pallas_call | solution.py:394
  39.1 0.1 collective-permute-start.3
  39.2 2.4 %collective-permute-start.4 = (f32[256,128]{1,0:T(8,128)S(1)}, f32[256,128]{1,0:T(8,128)S(1)}, u32[]{:S(2)}, u32[]{:S(2)}) collective-permute-start(f32[256,128]{1,0:T(8,128)S(1)} %get-tuple-element.29), channel_id=1, source_target_pairs={{0,30},{1,31},{2,4},{3,5},{4,2},{5,3},{6,8},{7,9},{8,6},{9,7},{10,... | collective-permute-start | bytes 393224 | tf_op jit(solution)/shard_map/ppermute | solution.py:62
  41.6 1.5 %collective-permute-start.5 = (f32[256,128]{1,0:T(8,128)S(1)}, f32[256,128]{1,0:T(8,128)S(1)}, u32[]{:S(2)}, u32[]{:S(2)}) collective-permute-start(f32[256,128]{1,0:T(8,128)S(1)} %get-tuple-element.30), channel_id=1, source_target_pairs={{0,1},{1,0},{2,3},{3,2},{4,5},{5,4},{6,7},{7,6},{8,9},{9,8},{10,11... | collective-permute-start | bytes 393224 | tf_op jit(solution)/shard_map/ppermute | solution.py:62
  43.2 0.0 collective-permute-done.3.rest_0_
  43.2 3.2 %collective-permute-done.4.rest_1_ = f32[256,128]{1,0:T(8,128)S(1)} collective-permute-done((f32[256,128]{1,0:T(8,128)S(1)}, f32[256,128]{1,0:T(8,128)S(1)}, u32[]{:S(2)}, u32[]{:S(2)}) %collective-permute-start.4) | collective-permute-done | bytes 131104 | tf_op jit(solution)/shard_map/ppermute | solution.py:62
  46.4 0.2 collective-permute-done.5.rest_2_
  46.6 4.4 %step1.1 = (f32[1536,128]{1,0:T(8,128)}, f32[1536,128]{1,0:T(8,128)S(1)}, f32[256,128]{1,0:T(8,128)S(1)}, f32[256,128]{1,0:T(8,128)S(1)}, f32[256,128]{1,0:T(8,128)S(1)}) custom-call(s32[6]{0:T(128)S(1)} %bitcast.12, s32[6]{0:T(128)S(1)} %bitcast.17, bf16[1536,1536]{1,0:T(8,128)(2,1)S(1)} %get-tuple-element.20.s_high, ...), custom_call_target="tpu_custom_call" | custom-call | tf_op jit(solution)/shard_map/step1/pallas_call | solution.py:394
  51.0 0.0 collective-permute-start.6
  51.0 3.0 %collective-permute-start.7 = (f32[256,128]{1,0:T(8,128)S(1)}, f32[256,128]{1,0:T(8,128)S(1)}, u32[]{:S(2)}, u32[]{:S(2)}) collective-permute-start(f32[256,128]{1,0:T(8,128)S(1)} %get-tuple-element.36), channel_id=1, source_target_pairs={{0,30},{1,31},{2,4},{3,5},{4,2},{5,3},{6,8},{7,9},{8,6},{9,7},{10,... | collective-permute-start | bytes 393224 | tf_op jit(solution)/shard_map/ppermute | solution.py:62
  54.0 0.6 %collective-permute-start.8 = (f32[256,128]{1,0:T(8,128)S(1)}, f32[256,128]{1,0:T(8,128)S(1)}, u32[]{:S(2)}, u32[]{:S(2)}) collective-permute-start(f32[256,128]{1,0:T(8,128)S(1)} %get-tuple-element.37), channel_id=1, source_target_pairs={{0,1},{1,0},{2,3},{3,2},{4,5},{5,4},{6,7},{7,6},{8,9},{9,8},{10,11... | collective-permute-start | bytes 393224 | tf_op jit(solution)/shard_map/ppermute | solution.py:62
  54.7 0.0 collective-permute-done.6.rest_0_
  54.7 3.4 %collective-permute-done.7.rest_1_ = f32[256,128]{1,0:T(8,128)S(1)} collective-permute-done((f32[256,128]{1,0:T(8,128)S(1)}, f32[256,128]{1,0:T(8,128)S(1)}, u32[]{:S(2)}, u32[]{:S(2)}) %collective-permute-start.7) | collective-permute-done | bytes 131104 | tf_op jit(solution)/shard_map/ppermute | solution.py:62
  58.1 0.9 %collective-permute-done.8.rest_2_ = f32[256,128]{1,0:T(8,128)S(1)} collective-permute-done((f32[256,128]{1,0:T(8,128)S(1)}, f32[256,128]{1,0:T(8,128)S(1)}, u32[]{:S(2)}, u32[]{:S(2)}) %collective-permute-start.8) | collective-permute-done | bytes 131104 | tf_op jit(solution)/shard_map/ppermute | solution.py:62
  59.0 1.5 %final.1 = f32[1536,128]{1,0:T(8,128)} custom-call(s32[6]{0:T(128)S(1)} %bitcast.13, f32[1536,128]{1,0:T(8,128)S(1)} %get-tuple-element.34.part, f32[256,128]{1,0:T(8,128)S(1)} %collective-permute-done.6.rest_0_, f32[256,128]{1,0:T(8,128)S(1)} %collective-permute-done.7.rest_1_, f32[256,128]{1,0:T(8,128)S(1)} %collective-permute-done.8.rest_2_), custom_call_target="tpu_custom_call" | custom-call | tf_op jit(solution)/shard_map/final/pallas_call | solution.py:405
Async XLA Ops:
  3.7 15.5 %collective-permute-start = (f32[256,384]{1,0:T(8,128)}, f32[256,384]{1,0:T(8,128)S(1)}, u32[]{:S(2)}, u32[]{:S(2)}) collective-permute-start(f32[256,384]{1,0:T(8,128)} %get-tuple-element.23), channel_id=1, source_target_pairs={{0,2},{1,3},{2,0},{3,1},{4,6},{5,7},{6,4},{7,5},{8,10},{9,11},{10,... | collective-permute-start | bytes 1179656 | tf_op jit(solution)/shard_map/ppermute | solution.py:62
  4.2 15.0 %collective-permute-start.1 = (f32[256,384]{1,0:T(8,128)}, f32[256,384]{1,0:T(8,128)S(1)}, u32[]{:S(2)}, u32[]{:S(2)}) collective-permute-start(f32[256,384]{1,0:T(8,128)} %get-tuple-element.24), channel_id=1, source_target_pairs={{0,30},{1,31},{2,4},{3,5},{4,2},{5,3},{6,8},{7,9},{8,6},{9,7},{10,... | collective-permute-start | bytes 1179656 | tf_op jit(solution)/shard_map/ppermute | solution.py:62
  9.8 9.4 %copy-start.1 = (s32[1,1,6]{2,1,0:T(1,128)S(1)}, s32[1,1,6]{2,1,0:T(1,128)}, u32[]{:S(2)}) copy-start(s32[1,1,6]{2,1,0:T(1,128)} %param.7) | copy-start | bytes 76
  9.8 9.4 %copy-start.2 = (s32[1,1,6]{2,1,0:T(1,128)S(1)}, s32[1,1,6]{2,1,0:T(1,128)}, u32[]{:S(2)}) copy-start(s32[1,1,6]{2,1,0:T(1,128)} %param.6) | copy-start | bytes 76
  9.8 25.5 %copy-start = (f32[1,1,1536,128]{3,2,1,0:T(8,128)S(1)}, f32[1,1,1536,128]{3,2,1,0:T(8,128)}, u32[]{:S(2)}) copy-start(f32[1,1,1536,128]{3,2,1,0:T(8,128)} %param.5) | copy-start | bytes 2359300
  9.8 9.3 %collective-permute-start.2 = (f32[256,384]{1,0:T(8,128)}, f32[256,384]{1,0:T(8,128)S(1)}, u32[]{:S(2)}, u32[]{:S(2)}) collective-permute-start(f32[256,384]{1,0:T(8,128)} %get-tuple-element.25), channel_id=1, source_target_pairs={{0,1},{1,0},{2,3},{3,2},{4,5},{5,4},{6,7},{7,6},{8,9},{9,8},{10,11... | collective-permute-start | bytes 1179656 | tf_op jit(solution)/shard_map/ppermute | solution.py:62
  39.1 4.0 %collective-permute-start.3 = (f32[256,128]{1,0:T(8,128)S(1)}, f32[256,128]{1,0:T(8,128)S(1)}, u32[]{:S(2)}, u32[]{:S(2)}) collective-permute-start(f32[256,128]{1,0:T(8,128)S(1)} %get-tuple-element.28), channel_id=1, source_target_pairs={{0,2},{1,3},{2,0},{3,1},{4,6},{5,7},{6,4},{7,5},{8,10},{9,11},{10,... | collective-permute-start | bytes 393224 | tf_op jit(solution)/shard_map/ppermute | solution.py:62
  39.2 7.2 %collective-permute-start.4 = (f32[256,128]{1,0:T(8,128)S(1)}, f32[256,128]{1,0:T(8,128)S(1)}, u32[]{:S(2)}, u32[]{:S(2)}) collective-permute-start(f32[256,128]{1,0:T(8,128)S(1)} %get-tuple-element.29), channel_id=1, source_target_pairs={{0,30},{1,31},{2,4},{3,5},{4,2},{5,3},{6,8},{7,9},{8,6},{9,7},{10,... | collective-permute-start | bytes 393224 | tf_op jit(solution)/shard_map/ppermute | solution.py:62
  41.6 5.0 %collective-permute-start.5 = (f32[256,128]{1,0:T(8,128)S(1)}, f32[256,128]{1,0:T(8,128)S(1)}, u32[]{:S(2)}, u32[]{:S(2)}) collective-permute-start(f32[256,128]{1,0:T(8,128)S(1)} %get-tuple-element.30), channel_id=1, source_target_pairs={{0,1},{1,0},{2,3},{3,2},{4,5},{5,4},{6,7},{7,6},{8,9},{9,8},{10,11... | collective-permute-start | bytes 393224 | tf_op jit(solution)/shard_map/ppermute | solution.py:62
  51.0 3.7 %collective-permute-start.6 = (f32[256,128]{1,0:T(8,128)S(1)}, f32[256,128]{1,0:T(8,128)S(1)}, u32[]{:S(2)}, u32[]{:S(2)}) collective-permute-start(f32[256,128]{1,0:T(8,128)S(1)} %get-tuple-element.35), channel_id=1, source_target_pairs={{0,2},{1,3},{2,0},{3,1},{4,6},{5,7},{6,4},{7,5},{8,10},{9,11},{10,... | collective-permute-start | bytes 393224 | tf_op jit(solution)/shard_map/ppermute | solution.py:62
  51.0 7.1 %collective-permute-start.7 = (f32[256,128]{1,0:T(8,128)S(1)}, f32[256,128]{1,0:T(8,128)S(1)}, u32[]{:S(2)}, u32[]{:S(2)}) collective-permute-start(f32[256,128]{1,0:T(8,128)S(1)} %get-tuple-element.36), channel_id=1, source_target_pairs={{0,30},{1,31},{2,4},{3,5},{4,2},{5,3},{6,8},{7,9},{8,6},{9,7},{10,... | collective-permute-start | bytes 393224 | tf_op jit(solution)/shard_map/ppermute | solution.py:62
  54.0 5.0 %collective-permute-start.8 = (f32[256,128]{1,0:T(8,128)S(1)}, f32[256,128]{1,0:T(8,128)S(1)}, u32[]{:S(2)}, u32[]{:S(2)}) collective-permute-start(f32[256,128]{1,0:T(8,128)S(1)} %get-tuple-element.37), channel_id=1, source_target_pairs={{0,1},{1,0},{2,3},{3,2},{4,5},{5,4},{6,7},{7,6},{8,9},{9,8},{10,11... | collective-permute-start | bytes 393224 | tf_op jit(solution)/shard_map/ppermute | solution.py:62

commit v3 on v2

v3 whole, which is shorter than its diff:
```python
import functools

import jax
import jax.numpy as jnp
from jax import lax
from jax.experimental import pallas as pl
from jax.experimental.pallas import tpu as pltpu
from jax.sharding import PartitionSpec as P

ITERS = 2
OMEGA = 0.6

SLOTS = 6
LANES = 128
OUTER = 32
MICRO = 8
F32 = jnp.float32
BF16 = jnp.bfloat16
SMEM = pl.BlockSpec(memory_space=pltpu.SMEM)
VMEM = pl.BlockSpec(memory_space=pltpu.VMEM)
HBM = pl.BlockSpec(memory_space=pltpu.HBM)


def face_list(mesh):
    met, alone = [], []
    for axis, turn in (("wide", 1), ("depth", 0), ("depth", 1), ("wide", 0)):
        (met if mesh.shape[axis] > 1 + turn else alone).append((axis, turn))
    return met + alone + [4, 5], len(met)


def face_slot(mesh, dirs_ref, face):
    there = False
    if isinstance(face, int):
        facing = face
    else:
        axis, turn = face
        index = lax.axis_index(axis)
        upper = (index + turn) % 2 == 0
        facing = jnp.where(upper, 1, 0) + (0 if axis == "wide" else 2)
        there = jnp.where(upper, index + 1 < mesh.shape[axis], index > 0)
    slot = jnp.int32(0)
    for k in range(SLOTS):
        slot = slot + jnp.where(dirs_ref[k] == facing, k, 0)
    return slot, there


def exchange(mesh, face, value):
    axis, turn = face
    other = "depth" if axis == "wide" else "wide"
    count, lines = mesh.shape[axis], mesh.shape[other]
    low = range(turn, count - 1, 2)
    met = {i + more for i in low for more in (0, 1)}
    pairs = [((i, line), (i + 1, line)) for i in low for line in range(lines)]
    alone = [(i, line) for i in range(count) if i not in met for line in range(lines)]
    pairs += list(zip(alone[::2], alone[1::2]))

    def flat(spot):
        place = {axis: spot[0], other: spot[1]}
        return place["wide"] * mesh.shape["depth"] + place["depth"]

    perm = [(flat(a), flat(b)) for a, b in pairs]
    perm += [(b, a) for a, b in perm]
    return lax.ppermute(value, ("wide", "depth"), sorted(perm))


def spread_row(x, k):
    return jnp.broadcast_to(x[k : k + 1, :], x.shape)


def tree_sum(terms):
    while len(terms) > 1:
        terms = [terms[i] + terms[i + 1] if i + 1 < len(terms) else terms[i] for i in range(0, len(terms), 2)]
    return terms[0]


def invert_diagonal(d, fill=lambda: None):
    rows, packs = len(d), len(d[0])
    lane = lax.broadcasted_iota(jnp.int32, (MICRO, LANES), 1)
    sub = lax.broadcasted_iota(jnp.int32, (MICRO, LANES), 0)
    half = lane - (lane & (OUTER - 1))
    local = lane & (OUTER - 1)
    for q in range(rows):
        own = (local >= q * MICRO) & (local < (q + 1) * MICRO)
        spots = [half + (q * MICRO + j) for j in range(MICRO)]
        cols = [[jnp.take_along_axis(d[q][p], spots[j], axis=1) for j in range(MICRO)] for p in range(packs)]
        scales = [[None] * MICRO for _ in range(packs)]
        for k in range(MICRO):
            pivot_row = sub == k
            for p in range(packs):
                c = cols[p]
                scale = 1.0 / spread_row(c[k], k)
                scales[p][k] = scale
                h = jnp.where(pivot_row, 0.0, c[k]) * scale
                for j in range(MICRO):
                    if j != k:
                        c[j] = c[j] - h * spread_row(c[j], k)
                c[k] = jnp.where(pivot_row, 1.0, -h)
            if k % 2:
                fill()
        for p in range(packs):
            scale = scales[p][0]
            for k in range(1, MICRO):
                scale = jnp.where(sub == k, scales[p][k], scale)
            row = jnp.where(own, jnp.where(local == sub + q * MICRO, 1.0, 0.0), d[q][p])
            row = tree_sum([cols[p][j] * spread_row(row, j) for j in range(MICRO)]) * scale
            spread = [spread_row(row, j) for j in range(MICRO)]
            for step in range(1, rows):
                i = (q + step) % rows
                x = d[i][p]
                change = tree_sum([jnp.take_along_axis(x, spots[j], axis=1) * spread[j] for j in range(MICRO)])
                d[i][p] = jnp.where(own, 0.0, x) - change
            d[q][p] = row
    return d


def split(x):
    high = x.astype(BF16)
    return high, (x - high.astype(F32)).astype(BF16)


def left(x):
    return jnp.concatenate(split(x), 1)


def right(x):
    high, low = split(x)
    return jnp.concatenate([jnp.concatenate([high, low], 1), jnp.concatenate([high, jnp.zeros_like(low)], 1)], 0)


def product(one, two):
    both = jnp.dot(one, two, preferred_element_type=F32)
    half = both.shape[1] // 2
    return both[:, :half] + both[:, half:]


def lane_group(rows):
    return lax.broadcasted_iota(jnp.int32, (rows, LANES), 1) // OUTER


def packed(a_ref, rows, cl, s, fill=0.0):
    groups = LANES // OUTER
    height = rows.stop - rows.start
    group = lane_group(height)
    out = []
    for first in range(0, a_ref.shape[0], groups):
        pack = None
        for g in range(first, min(a_ref.shape[0], first + groups)):
            to = g - first
            x = a_ref[g, rows, cl]
            if to != s:
                x = pltpu.roll(x, ((to - s) * OUTER) % LANES, 1)
            pack = x if pack is None else jnp.where(group >= to, x, pack)
        if to + 1 < groups:
            spare = jnp.zeros_like(pack)
            if fill:
                spare = jnp.where(lax.broadcasted_iota(jnp.int32, pack.shape, 1) % OUTER == lax.broadcasted_iota(jnp.int32, pack.shape, 0), fill, spare)
            pack = jnp.where(group > to, spare, pack)
        out.append(pack)
    return out


def block_diagonal(x):
    group = lane_group(OUTER)
    return jnp.concatenate([jnp.where(group == k, x, 0.0) for k in range(LANES // OUTER)], 0)


def tile_update(a_ref, rl, cl, s, packs):
    groups = LANES // OUTER
    group_row, group_all = lane_group(OUTER), lane_group(LANES)
    band = slice(rl.start + s * OUTER, rl.start + (s + 1) * OUTER)
    count = a_ref.shape[0]

    def first(g):
        p, at = divmod(g, groups)
        w = packs[p]
        if at != s:
            w = pltpu.roll(w, ((s - at) * OUTER) % LANES, 1)
        w = jnp.where(group_row == s, w, 0.0)
        t = a_ref[g, rl, cl]
        return w, t, product(left(w), right(t))

    def second(g, w, t, row):
        row = jnp.where(group_row == s, w, row)
        parts = [jnp.zeros((OUTER, LANES), F32)] * groups
        parts[s] = row
        change = product(left(t), right(jnp.concatenate(parts, 0)))
        return t, row, change

    def third(g, t, row, change):
        a_ref[g, rl, cl] = jnp.where(group_all == s, 0.0, t) - change
        a_ref[g, band, cl] = row

    one, two = {}, {}
    for step in range(count + 2):
        if step < count:
            one[step] = first(step)
            yield
        if 0 <= step - 1 < count:
            two[step - 1] = second(step - 1, *one.pop(step - 1))
            yield
        if 0 <= step - 2 < count:
            third(step - 2, *two.pop(step - 2))
            yield


def invert_tile(a_ref, rl, cl):
    groups = LANES // OUTER
    pieces = OUTER // MICRO
    bands = [slice(rl.start + s * OUTER, rl.start + (s + 1) * OUTER) for s in range(groups)]
    d = packed(a_ref, bands[0], cl, 0, 1.0)
    rest = iter(())
    for s in range(groups):
        lines = [[x[i * MICRO : (i + 1) * MICRO] for x in d] for i in range(pieces)]
        lines = invert_diagonal(lines, lambda: next(rest, None))
        for _ in rest:
            pass
        packs = [jnp.concatenate([lines[i][p] for i in range(pieces)], 0) for p in range(len(d))]
        if s + 1 < groups:
            ahead = packed(a_ref, bands[s], cl, s + 1)
            below = packed(a_ref, bands[s + 1], cl, s)
            d = packed(a_ref, bands[s + 1], cl, s + 1, 1.0)
            rows = [product(left(w), right(block_diagonal(ahead[p]))) for p, w in enumerate(packs)]
            changes = [product(left(below[p]), right(block_diagonal(row))) for p, row in enumerate(rows)]
            d = [x - change for x, change in zip(d, changes)]
        rest = tile_update(a_ref, rl, cl, s, packs)
    for _ in rest:
        pass


def invert_blocks(a_ref):
    count, size = a_ref.shape[0], a_ref.shape[-1]
    tiles = [slice(b * LANES, (b + 1) * LANES) for b in range(size // LANES)]
    for own in tiles:
        invert_tile(a_ref, own, own)
        others = [t for t in tiles if t is not own]
        lefts = [left(a_ref[g, own, own]) for g in range(count)]
        rights = [right(a_ref[g, own, own]) for g in range(count)]
        columns = [[left(a_ref[g, t, own]) for t in others] for g in range(count)]
        rows = [[product(lefts[g], right(a_ref[g, own, t])) for t in others] for g in range(count)]
        for g in range(count):
            for i, ti in enumerate(others):
                a_ref[g, ti, own] = -product(columns[g][i], rights[g])
        for g in range(count):
            for j, tj in enumerate(others):
                a_ref[g, own, tj] = rows[g][j]
                row = right(rows[g][j])
                for i, ti in enumerate(others):
                    a_ref[g, ti, tj] = a_ref[g, ti, tj] - product(columns[g][i], row)


def slot_rows(slot, rows):
    return pl.ds(pl.multiple_of(slot * rows, rows), rows)


def row_mask(rows, size, lanes=LANES):
    return lax.broadcasted_iota(jnp.int32, (rows, lanes), 0) < size


def corner(size):
    row = lax.broadcasted_iota(jnp.int32, (size, size), 0)
    return row, lax.broadcasted_iota(jnp.int32, (size, size), 1)


def pack_kernel(mesh, faces, many, dirs, matrix, *rest):
    outs, (block, sems) = rest[:many], rest[many:]
    rows = block.shape[1]
    half = rows // 2
    copies = []
    for n in range(many):
        slot, _ = face_slot(mesh, dirs, faces[n])
        at = slot_rows(slot, rows)
        copies.append(pltpu.make_async_copy(matrix.at[at, at], block.at[n], sems.at[n]))
        copies[-1].start()
    row, col = corner(half)
    for n in range(many):
        copies[n].wait()
        last = block[n, half:, half:]
        outs[n][:half, :] = jnp.where(row >= col, block[n, :half, :half], last)
        outs[n][half:rows, :] = block[n, half:, :half]
        diagonal = jnp.where(row == col, last, 0.0).sum(axis=0, keepdims=True)
        outs[n][rows:, :] = jnp.broadcast_to(diagonal, (outs[n].shape[0] - rows, half))


def unpacked(packed_ref, rows):
    half = rows // 2
    row, col = corner(half)
    fold = packed_ref[:half, :]
    turned = fold.T
    low = packed_ref[half:rows, :]
    diagonal = jnp.broadcast_to(packed_ref[rows : rows + 1, :], (half, half))
    first = jnp.where(row >= col, fold, turned)
    last = jnp.where(row < col, fold, jnp.where(row > col, turned, diagonal))
    return first, low.T, low, last


def split_kernel(mesh, faces, many, dirs, matrix, loads, high_ref, low_ref, diagonal, *rest):
    outs, (buffer, sems, load_sem) = rest[:many], rest[many:]
    order = matrix.shape[0]
    rows = diagonal.shape[1]
    depth, chunk = buffer.shape[:2]
    total = order // chunk

    def copy(n):
        return pltpu.make_async_copy(matrix.at[pl.ds(n * chunk, chunk), :], buffer.at[n % depth], sems.at[n % depth])

    for n in range(min(depth, total)):
        copy(n).start()
    copies = []
    for n in range(many):
        slot, _ = face_slot(mesh, dirs, faces[n])
        copies.append(pltpu.make_async_copy(loads.at[slot_rows(slot, rows), :], outs[n], load_sem.at[n]))
        copies[-1].start()
    for n in range(total):
        copy(n).wait()
        at = slice(n * chunk, (n + 1) * chunk)
        high, low = split(buffer[n % depth])
        high_ref[at, :] = high
        low_ref[at, :] = low
        k, start = divmod(n * chunk, rows)
        diagonal[k, start : start + chunk, :] = buffer[n % depth, :, k * rows : (k + 1) * rows]
        if n + depth < total:
            copy(n + depth).start()
    for one in copies:
        one.wait()


def inverse_kernel(mesh, faces, many, dirs, sizes, diagonal, *rest):
    got, (high_ref, low_ref, work) = rest[:many], rest[many:]
    rows = work.shape[-1]
    half = rows // 2
    work[...] = diagonal[...]
    for n in range(many):
        slot, there = face_slot(mesh, dirs, faces[n])
        factor = jnp.where(there, 1.0, 0.0)
        parts = unpacked(got[n], rows)
        for k, part in enumerate(parts):
            i, j = divmod(k, 2)
            at = (slot, slice(i * half, (i + 1) * half), slice(j * half, (j + 1) * half))
            work[at] = work[at] + factor * part
    row, col = corner(rows)
    for k in range(SLOTS):
        used = jnp.maximum(row, col) < sizes[k]
        work[k] = jnp.where(used, work[k], jnp.where(row == col, 1.0, 0.0))
    invert_blocks(work)
    for k in range(SLOTS):
        high_ref[k], low_ref[k] = split(work[k])


def apply_face(slot, sizes, s_high, s_low, pair, loads, out):
    rows, cases = out.shape
    at = slot_rows(slot, rows)
    both = jnp.dot(s_high[at, :], pair[...], preferred_element_type=F32)
    both += jnp.dot(s_low[at, :], pair[...], preferred_element_type=F32)
    value = loads[at, :] - (both[:, :cases] + both[:, cases:])
    out[...] = jnp.where(row_mask(rows, sizes[slot], cases), value, 0.0)


def lead_kernel(mesh, faces, many, first, dirs, sizes, s_high, s_low, i_high, i_low, loads, *rest):
    got, rest = rest[:many], rest[many:]
    before = parts = None
    if not first:
        before, parts, rest = rest[0], rest[1 : 1 + len(faces)], rest[1 + len(faces) :]
    disp, pair, out = rest
    rows, cases = out.shape
    for n, face in enumerate(faces):
        slot, there = face_slot(mesh, dirs, face)
        at = slot_rows(slot, rows)
        if first:
            value = loads[at, :]
        else:
            value = parts[n][...]
        if n < many:
            value = value + jnp.where(there, 1.0, 0.0) * got[n][...]
        if first:
            value = jnp.where(row_mask(rows, sizes[slot], cases), value, 0.0)
        both = jnp.concatenate(split(value), 1)
        update = jnp.dot(i_high[slot], both, preferred_element_type=F32)
        update += jnp.dot(i_low[slot], both, preferred_element_type=F32)
        value = OMEGA * (update[:, :cases] + update[:, cases:])
        if before is not None:
            value = before[at, :] + value
        disp[at, :] = value
        pair[at, :cases], pair[at, cases:] = split(value)
    slot, _ = face_slot(mesh, dirs, faces[0])
    apply_face(slot, sizes, s_high, s_low, pair, loads, out)


def more_kernel(mesh, some, dirs, sizes, s_high, s_low, pair, loads, *outs):
    for face, out in zip(some, outs):
        slot, _ = face_slot(mesh, dirs, face)
        apply_face(slot, sizes, s_high, s_low, pair, loads, out)


def final_kernel(mesh, faces, many, dirs, *rest):
    parts, got, out = rest[: len(faces)], rest[len(faces) : len(faces) + many], rest[-1]
    rows = parts[0].shape[0]
    for n, face in enumerate(faces):
        slot, there = face_slot(mesh, dirs, face)
        value = parts[n][...]
        if n < many:
            value = value + jnp.where(there, 1.0, 0.0) * got[n][...]
        out[slot_rows(slot, rows), :] = value


def params(mib, **kw):
    return pltpu.CompilerParams(vmem_limit_bytes=mib << 20, **kw)


def shape(*dims, dtype=F32):
    return jax.ShapeDtypeStruct(dims, dtype)


def cost(flops, touched=0):
    return pl.CostEstimate(flops=flops, bytes_accessed=touched, transcendentals=0)


def local(mesh, schur, loads, face_sizes, face_dir):
    matrix = schur[0, 0]
    load = loads[0, 0]
    sizes = face_sizes[0, 0]
    dirs = face_dir[0, 0]
    order, cases = load.shape
    rows = order // SLOTS
    faces, many = face_list(mesh)

    def swap(sends):
        return [exchange(mesh, face, value) for face, value in zip(faces[:many], sends)]

    blocks = pl.pallas_call(
        functools.partial(pack_kernel, mesh, faces, many),
        name="pack",
        out_shape=[shape(rows + 8, rows // 2)] * many,
        in_specs=[SMEM, HBM],
        out_specs=[VMEM] * many,
        scratch_shapes=[pltpu.VMEM((many, rows, rows), F32), pltpu.SemaphoreType.DMA((many,))],
        compiler_params=params(56),
    )(dirs, matrix)
    blocks = swap(blocks)

    chunk, ahead = rows // 2, 6
    s_high, s_low, diagonal, *sends = pl.pallas_call(
        functools.partial(split_kernel, mesh, faces, many),
        name="split",
        out_shape=[shape(order, order, dtype=BF16)] * 2 + [shape(SLOTS, rows, rows)] + [shape(rows, cases)] * many,
        in_specs=[SMEM, HBM, HBM],
        out_specs=[VMEM] * (3 + many),
        scratch_shapes=[pltpu.VMEM((ahead, chunk, order), F32), pltpu.SemaphoreType.DMA((ahead,)), pltpu.SemaphoreType.DMA((many,))],
        compiler_params=params(40),
        cost_estimate=cost(4 * order * order, 4 * order * order),
    )(dirs, matrix, load)
    got = swap(sends)

    i_high, i_low = pl.pallas_call(
        functools.partial(inverse_kernel, mesh, faces, many),
        name="inverse",
        out_shape=[shape(SLOTS, rows, rows, dtype=BF16)] * 2,
        in_specs=[SMEM, SMEM, VMEM] + [VMEM] * many,
        out_specs=[VMEM] * 2,
        scratch_shapes=[pltpu.VMEM((SLOTS, rows, rows), F32)],
        compiler_params=params(16),
        cost_estimate=cost(2 * SLOTS * rows**3 * 40),
    )(dirs, sizes, diagonal, *blocks)

    disp = parts = None
    for step in range(ITERS):
        first = step == 0
        args = [dirs, sizes, s_high, s_low, i_high, i_low, load, *got] + ([] if first else [disp, *parts])
        disp, pair, part = pl.pallas_call(
            functools.partial(lead_kernel, mesh, faces, many, first),
            name=f"lead{step}",
            out_shape=[shape(order, cases), shape(order, 2 * cases, dtype=BF16), shape(rows, cases)],
            in_specs=[SMEM, SMEM] + [VMEM] * (len(args) - 2),
            out_specs=[VMEM] * 3,
            compiler_params=params(16),
            cost_estimate=cost(6 * rows * order * cases),
        )(*args)
        parts = [part]
        while len(parts) < SLOTS:
            at = len(parts)
            some = faces[at : at + 1] if at < many else faces[at:]
            parts += pl.pallas_call(
                functools.partial(more_kernel, mesh, some),
                name=f"more{step}",
                out_shape=[shape(rows, cases)] * len(some),
                in_specs=[SMEM, SMEM] + [VMEM] * 4,
                out_specs=[VMEM] * len(some),
                compiler_params=params(16),
                cost_estimate=cost(6 * rows * order * cases * len(some)),
            )(dirs, sizes, s_high, s_low, pair, load)
        got = swap(parts)

    final = pl.pallas_call(
        functools.partial(final_kernel, mesh, faces, many),
        name="final",
        out_shape=shape(order, cases),
        in_specs=[SMEM] + [VMEM] * (SLOTS + many),
        out_specs=VMEM,
        compiler_params=params(8),
    )(dirs, *parts, *got)
    return disp[None, None], final[None, None]


def solution(mesh):
    return jax.shard_map(
        functools.partial(local, mesh),
        mesh=mesh,
        in_specs=(
            P("wide", "depth", None, None),
            P("wide", "depth", None, None),
            P("wide", "depth", None),
            P("wide", "depth", None),
        ),
        out_specs=(P("wide", "depth", None, None), P("wide", "depth", None, None)),
        check_vma=False,
    )
```

time: 60.8 us -> 54.8 us (0.901)
  starting transfers between devices: 15.4 us -> 10.9 us
  waiting for transfers between devices: 7.79 us -> 5.55 us
  Pallas kernels: 36.6 us -> 37.4 us
    ppermute x9 -> x12, starting transfers between devices: 15.4 us -> 10.9 us  [exchange(): return lax.ppermute(value, ('wide', 'depth'), sorted(perm))]
    ppermute x9 -> x12, waiting for transfers between devices: 7.79 us -> 5.55 us  [exchange(): return lax.ppermute(value, ('wide', 'depth'), sorted(perm))]
    pallas_call x6 -> x12, Pallas kernels: 36.6 us -> 37.4 us  [the longest x1 14.3 us: local(): pl.pallas_call(functools.partial(inverse_kernel, mesh, faces, many), name...]
  transfers between devices with their start and end apart: 9 -> 12, of which waited for: 4 -> 4; matrix products, arithmetic and copies ran while one was open for 0% -> 0% of each run, Pallas kernels for 13% -> 42%
where the time goes in v3:
time: 54.8 us; the launch traced here: 54.6 us
  Pallas kernels  37.4 us (68%)
  starting transfers between devices  10.9 us (20%)
  waiting for transfers between devices  5.55 us (10%)
  between operations  0.77 us (1%)
    pallas_call x1, Pallas kernels, local(): pl.pallas_call(functools.partial(inverse_kernel, mesh, faces, many), name...  14.3 us
    ppermute x12, starting transfers between devices, exchange(): return lax.ppermute(value, ('wide', 'depth'), sorted(perm))  10.9 us
    pallas_call x6, Pallas kernels, local(): pl.pallas_call(functools.partial(more_kernel, mesh, some), name=f'more{st...  8.3 us
    pallas_call x2, Pallas kernels, local(): pl.pallas_call(functools.partial(lead_kernel, mesh, faces, many, first),...  5.86 us
    ppermute x12, waiting for transfers between devices, exchange(): return lax.ppermute(value, ('wide', 'depth'), sorted(perm))  5.55 us
    pallas_call x1, Pallas kernels, local(): pl.pallas_call(functools.partial(split_kernel, mesh, faces, many), name='...  4.67 us
    pallas_call x1, Pallas kernels, local(): pl.pallas_call(functools.partial(pack_kernel, mesh, faces, many), name='p...  2.71 us
    pallas_call x1, Pallas kernels, local(): pl.pallas_call(functools.partial(final_kernel, mesh, faces, many), name='...  1.54 us
  transfers between devices with their start and end apart: 12, of which 4 were waited for; matrix products, arithmetic and copies ran while one was open for 0% of the time, Pallas kernels for 42%

profile of v3, /device:TPU:0, one launch (start us, length us, event | category | flops | bytes accessed | tf_op | source)
XLA Modules:
  0.0 54.6 jit_solution(10418978625314993663)
XLA Ops:
  0.6 0.0 copy-start
  0.6 0.0 copy-start.1
  0.6 2.7 %pack.1 = (f32[264,128]{1,0:T(8,128)}, f32[264,128]{1,0:T(8,128)}, f32[264,128]{1,0:T(8,128)}) custom-call(s32[6]{0:T(128)} %bitcast.15, f32[1536,1536]{1,0:T(8,128)} %bitcast.36), custom_call_target="tpu_custom_call" | custom-call | tf_op jit(solution)/shard_map/pack/pallas_call | solution.py:429
  3.4 3.1 %collective-permute-start = (f32[264,128]{1,0:T(8,128)}, f32[264,128]{1,0:T(8,128)S(1)}, u32[]{:S(2)}, u32[]{:S(2)}) collective-permute-start(f32[264,128]{1,0:T(8,128)} %get-tuple-element.28), channel_id=1, source_target_pairs={{0,1},{1,0},{2,4},{3,5},{4,2},{5,3},{6,8},{7,9},{8,6},{9,7},{10,12... | collective-permute-start | bytes 405512 | tf_op jit(solution)/shard_map/ppermute | solution.py:63
  6.4 0.1 collective-permute-start.1
  6.5 1.2 %collective-permute-start.2 = (f32[264,128]{1,0:T(8,128)}, f32[264,128]{1,0:T(8,128)S(1)}, u32[]{:S(2)}, u32[]{:S(2)}) collective-permute-start(f32[264,128]{1,0:T(8,128)} %get-tuple-element.30), channel_id=1, source_target_pairs={{0,2},{1,3},{2,0},{3,1},{4,6},{5,7},{6,4},{7,5},{8,10},{9,11},{10,... | collective-permute-start | bytes 405512 | tf_op jit(solution)/shard_map/ppermute | solution.py:63
  7.8 0.0 copy-done
  7.8 0.0 copy-done.1
  7.8 0.0 copy-start.2
  7.8 4.7 %split.1 = (bf16[1536,1536]{1,0:T(8,128)(2,1)S(1)}, bf16[1536,1536]{1,0:T(8,128)(2,1)S(1)}, f32[6,256,256]{2,1,0:T(8,128)S(1)}, f32[256,128]{1,0:T(8,128)S(1)}, ...) custom-call(s32[6]{0:T(128)S(1)} %bitcast.16, f32[1536,1536]{1,0:T(8,128)} %bitcast.37, f32[1536,128]{1,0:T(8,128)S(1)} %bitcast.6), custom_call_target="tpu_custom_call" | custom-call | flops 9437184 | bytes 9437184 | tf_op jit(solution)/shard_map/split/pallas_call | solution.py:441
  12.4 0.8 %collective-permute-start.3 = (f32[256,128]{1,0:T(8,128)S(1)}, f32[256,128]{1,0:T(8,128)S(1)}, u32[]{:S(2)}, u32[]{:S(2)}) collective-permute-start(f32[256,128]{1,0:T(8,128)S(1)} %get-tuple-element.33), channel_id=1, source_target_pairs={{0,1},{1,0},{2,4},{3,5},{4,2},{5,3},{6,8},{7,9},{8,6},{9,7},{10,12... | collective-permute-start | bytes 393224 | tf_op jit(solution)/shard_map/ppermute | solution.py:63
  13.2 1.3 %collective-permute-start.4 = (f32[256,128]{1,0:T(8,128)S(1)}, f32[256,128]{1,0:T(8,128)S(1)}, u32[]{:S(2)}, u32[]{:S(2)}) collective-permute-start(f32[256,128]{1,0:T(8,128)S(1)} %get-tuple-element.34), channel_id=1, source_target_pairs={{0,1},{1,0},{2,3},{3,2},{4,5},{5,4},{6,7},{7,6},{8,9},{9,8},{10,11... | collective-permute-start | bytes 393224 | tf_op jit(solution)/shard_map/ppermute | solution.py:63
  14.5 0.0 collective-permute-done.rest_0_
  14.5 0.0 collective-permute-start.5
  14.5 0.0 collective-permute-done.1.rest_1_
  14.5 0.0 collective-permute-done.2.rest_2_
  14.6 0.0 copy-done.2
  14.6 14.3 %inverse.1 = (bf16[6,256,256]{2,1,0:T(8,128)(2,1)S(1)}, bf16[6,256,256]{2,1,0:T(8,128)(2,1)S(1)}) custom-call(s32[6]{0:T(128)S(1)} %bitcast.17, s32[6]{0:T(128)S(1)} %bitcast.27, f32[6,256,256]{2,1,0:T(8,128)S(1)} %get-tuple-element.27.diagonal, f32[264,128]{1,0:T(8,128)S(1)} %collective-permute-done.rest_0_, f32[264,128]{1,0:T(8,128)S(1)} %collective-permute-done.1.rest_1_, ...), custom_call_target="tpu_custom_call" | custom-call | flops 8053063680 | tf_op jit(solution)/shard_map/inverse/pallas_call | solution.py:453
  28.9 0.0 collective-permute-done.3.rest_0_
  28.9 0.0 collective-permute-done.4.rest_1_
  28.9 0.0 collective-permute-done.5.rest_2_
  28.9 2.7 %lead0.1 = (f32[1536,128]{1,0:T(8,128)S(1)}, bf16[1536,256]{1,0:T(8,128)(2,1)S(1)}, f32[256,128]{1,0:T(8,128)S(1)}) custom-call(s32[6]{0:T(128)S(1)} %bitcast.18, s32[6]{0:T(128)S(1)} %bitcast.28, bf16[1536,1536]{1,0:T(8,128)(2,1)S(1)} %get-tuple-element.25.s_high, bf16[1536,1536]{1,0:T(8,128)(2,1)S(1)} %get-tuple-element.26.s_low, ...), custom_call_target="tpu_custom_call" | custom-call | flops 301989888 | tf_op jit(solution)/shard_map/lead0/pallas_call | solution.py:468
  31.6 1.1 %more0.4.rest_6_ = f32[256,128]{1,0:T(8,128)S(1)} custom-call(s32[6]{0:T(128)S(1)} %bitcast.19, s32[6]{0:T(128)S(1)} %bitcast.29, bf16[1536,1536]{1,0:T(8,128)(2,1)S(1)} %get-tuple-element.25.s_high, bf16[1536,1536]{1,0:T(8,128)(2,1)S(1)} %get-tuple-element.26.s_low, bf16[1536,256]{1,0:T(8,128)(2,1)S(1)} %get-tuple-element.37.pair, f32[1536,128]{1,0:T(8,128)S(1)} %bitcast.8), custom_call_target="tpu_custom_call" | custom-call | flops 301989888 | tf_op jit(solution)/shard_map/more0/pallas_call | solution.py:481
  32.7 1.1 %more0.3.rest_5_ = f32[256,128]{1,0:T(8,128)S(1)} custom-call(s32[6]{0:T(128)S(1)} %bitcast.20, s32[6]{0:T(128)S(1)} %bitcast.30, bf16[1536,1536]{1,0:T(8,128)(2,1)S(1)} %get-tuple-element.25.s_high, bf16[1536,1536]{1,0:T(8,128)(2,1)S(1)} %get-tuple-element.26.s_low, bf16[1536,256]{1,0:T(8,128)(2,1)S(1)} %get-tuple-element.37.pair, f32[1536,128]{1,0:T(8,128)S(1)} %bitcast.9), custom_call_target="tpu_custom_call" | custom-call | flops 301989888 | tf_op jit(solution)/shard_map/more0/pallas_call | solution.py:481
  33.8 1.4 %collective-permute-start.7 = (f32[256,128]{1,0:T(8,128)S(1)}, f32[256,128]{1,0:T(8,128)S(1)}, u32[]{:S(2)}, u32[]{:S(2)}) collective-permute-start(f32[256,128]{1,0:T(8,128)S(1)} %more0.3.rest_5_), channel_id=1, source_target_pairs={{0,1},{1,0},{2,3},{3,2},{4,5},{5,4},{6,7},{7,6},{8,9},{9,8},{10,11... | collective-permute-start | bytes 393224 | tf_op jit(solution)/shard_map/ppermute | solution.py:63
  35.3 0.0 collective-permute-start.8
  35.3 0.9 %collective-permute-start.6 = (f32[256,128]{1,0:T(8,128)S(1)}, f32[256,128]{1,0:T(8,128)S(1)}, u32[]{:S(2)}, u32[]{:S(2)}) collective-permute-start(f32[256,128]{1,0:T(8,128)S(1)} %get-tuple-element.36.rest_4_), channel_id=1, source_target_pairs={{0,1},{1,0},{2,4},{3,5},{4,2},{5,3},{6,8},{7,9},{8,6},{9,7},{10,12... | collective-permute-start | bytes 393224 | tf_op jit(solution)/shard_map/ppermute | solution.py:63
  36.1 1.9 %more0.5 = (f32[256,128]{1,0:T(8,128)S(1)}, f32[256,128]{1,0:T(8,128)S(1)}, f32[256,128]{1,0:T(8,128)S(1)}) custom-call(s32[6]{0:T(128)S(1)} %bitcast.21, s32[6]{0:T(128)S(1)} %bitcast.31, bf16[1536,1536]{1,0:T(8,128)(2,1)S(1)} %get-tuple-element.25.s_high, bf16[1536,1536]{1,0:T(8,128)(2,1)S(1)} %get-tuple-element.26.s_low, ...), custom_call_target="tpu_custom_call" | custom-call | flops 905969664 | tf_op jit(solution)/shard_map/more0/pallas_call | solution.py:481
  38.1 1.7 %collective-permute-done.7.rest_1_ = f32[256,128]{1,0:T(8,128)S(1)} collective-permute-done((f32[256,128]{1,0:T(8,128)S(1)}, f32[256,128]{1,0:T(8,128)S(1)}, u32[]{:S(2)}, u32[]{:S(2)}) %collective-permute-start.7) | collective-permute-done | bytes 131104 | tf_op jit(solution)/shard_map/ppermute | solution.py:63
  39.8 0.0 collective-permute-done.8.rest_2_
  39.8 1.4 %collective-permute-done.6.rest_0_ = f32[256,128]{1,0:T(8,128)S(1)} collective-permute-done((f32[256,128]{1,0:T(8,128)S(1)}, f32[256,128]{1,0:T(8,128)S(1)}, u32[]{:S(2)}, u32[]{:S(2)}) %collective-permute-start.6) | collective-permute-done | bytes 131104 | tf_op jit(solution)/shard_map/ppermute | solution.py:63
  41.2 3.2 %lead1.1 = (f32[1536,128]{1,0:T(8,128)}, bf16[1536,256]{1,0:T(8,128)(2,1)S(1)}, f32[256,128]{1,0:T(8,128)S(1)}) custom-call(s32[6]{0:T(128)S(1)} %bitcast.22, s32[6]{0:T(128)S(1)} %bitcast.32, bf16[1536,1536]{1,0:T(8,128)(2,1)S(1)} %get-tuple-element.25.s_high, bf16[1536,1536]{1,0:T(8,128)(2,1)S(1)} %get-tuple-element.26.s_low, ...), custom_call_target="tpu_custom_call" | custom-call | flops 301989888 | tf_op jit(solution)/shard_map/lead1/pallas_call | solution.py:468
  44.4 1.1 %more1.4.rest_2_ = f32[256,128]{1,0:T(8,128)S(1)} custom-call(s32[6]{0:T(128)S(1)} %bitcast.23, s32[6]{0:T(128)S(1)} %bitcast.33, bf16[1536,1536]{1,0:T(8,128)(2,1)S(1)} %get-tuple-element.25.s_high, bf16[1536,1536]{1,0:T(8,128)(2,1)S(1)} %get-tuple-element.26.s_low, bf16[1536,256]{1,0:T(8,128)(2,1)S(1)} %get-tuple-element.44.pair, f32[1536,128]{1,0:T(8,128)S(1)} %bitcast.12), custom_call_target="tpu_custom_call" | custom-call | flops 301989888 | tf_op jit(solution)/shard_map/more1/pallas_call | solution.py:481
  45.5 1.1 %more1.3.rest_1_ = f32[256,128]{1,0:T(8,128)S(1)} custom-call(s32[6]{0:T(128)S(1)} %bitcast.24, s32[6]{0:T(128)S(1)} %bitcast.34, bf16[1536,1536]{1,0:T(8,128)(2,1)S(1)} %get-tuple-element.25.s_high, bf16[1536,1536]{1,0:T(8,128)(2,1)S(1)} %get-tuple-element.26.s_low, bf16[1536,256]{1,0:T(8,128)(2,1)S(1)} %get-tuple-element.44.pair, f32[1536,128]{1,0:T(8,128)S(1)} %bitcast.13), custom_call_target="tpu_custom_call" | custom-call | flops 301989888 | tf_op jit(solution)/shard_map/more1/pallas_call | solution.py:481
  46.6 1.0 %collective-permute-start.10 = (f32[256,128]{1,0:T(8,128)S(1)}, f32[256,128]{1,0:T(8,128)S(1)}, u32[]{:S(2)}, u32[]{:S(2)}) collective-permute-start(f32[256,128]{1,0:T(8,128)S(1)} %more1.3.rest_1_), channel_id=1, source_target_pairs={{0,1},{1,0},{2,3},{3,2},{4,5},{5,4},{6,7},{7,6},{8,9},{9,8},{10,11... | collective-permute-start | bytes 393224 | tf_op jit(solution)/shard_map/ppermute | solution.py:63
  47.6 0.0 collective-permute-start.11
  47.6 1.1 %collective-permute-start.9 = (f32[256,128]{1,0:T(8,128)S(1)}, f32[256,128]{1,0:T(8,128)S(1)}, u32[]{:S(2)}, u32[]{:S(2)}) collective-permute-start(f32[256,128]{1,0:T(8,128)S(1)} %get-tuple-element.43.rest_0_), channel_id=1, source_target_pairs={{0,1},{1,0},{2,4},{3,5},{4,2},{5,3},{6,8},{7,9},{8,6},{9,7},{10,12... | collective-permute-start | bytes 393224 | tf_op jit(solution)/shard_map/ppermute | solution.py:63
  48.7 1.9 %more1.5 = (f32[256,128]{1,0:T(8,128)S(1)}, f32[256,128]{1,0:T(8,128)S(1)}, f32[256,128]{1,0:T(8,128)S(1)}) custom-call(s32[6]{0:T(128)S(1)} %bitcast.25, s32[6]{0:T(128)S(1)} %bitcast.35, bf16[1536,1536]{1,0:T(8,128)(2,1)S(1)} %get-tuple-element.25.s_high, bf16[1536,1536]{1,0:T(8,128)(2,1)S(1)} %get-tuple-element.26.s_low, ...), custom_call_target="tpu_custom_call" | custom-call | flops 905969664 | tf_op jit(solution)/shard_map/more1/pallas_call | solution.py:481
  50.6 1.0 %collective-permute-done.10.rest_7_ = f32[256,128]{1,0:T(8,128)S(1)} collective-permute-done((f32[256,128]{1,0:T(8,128)S(1)}, f32[256,128]{1,0:T(8,128)S(1)}, u32[]{:S(2)}, u32[]{:S(2)}) %collective-permute-start.10) | collective-permute-done | bytes 131104 | tf_op jit(solution)/shard_map/ppermute | solution.py:63
  51.6 0.0 collective-permute-done.11.rest_8_
  51.6 1.4 %collective-permute-done.9.rest_6_ = f32[256,128]{1,0:T(8,128)S(1)} collective-permute-done((f32[256,128]{1,0:T(8,128)S(1)}, f32[256,128]{1,0:T(8,128)S(1)}, u32[]{:S(2)}, u32[]{:S(2)}) %collective-permute-start.9) | collective-permute-done | bytes 131104 | tf_op jit(solution)/shard_map/ppermute | solution.py:63
  53.0 1.5 %final.1 = f32[1536,128]{1,0:T(8,128)} custom-call(s32[6]{0:T(128)S(1)} %bitcast.26, f32[256,128]{1,0:T(8,128)S(1)} %get-tuple-element.43.rest_0_, f32[256,128]{1,0:T(8,128)S(1)} %more1.3.rest_1_, f32[256,128]{1,0:T(8,128)S(1)} %more1.4.rest_2_, f32[256,128]{1,0:T(8,128)S(1)} %get-tuple-element.45.rest_3_, f32[256,128]{1,0:T(8,128)S(1)} %get-tuple-element.46.rest_4_, ...), custom_call_target="tpu_custom_call" | custom-call | tf_op jit(solution)/shard_map/final/pallas_call | solution.py:492
Async XLA Ops:
  0.6 7.1 %copy-start = (f32[1,1,1536,128]{3,2,1,0:T(8,128)S(1)}, f32[1,1,1536,128]{3,2,1,0:T(8,128)}, u32[]{:S(2)}) copy-start(f32[1,1,1536,128]{3,2,1,0:T(8,128)} %param.5) | copy-start | bytes 2359300
  0.6 7.1 %copy-start.1 = (s32[1,1,6]{2,1,0:T(1,128)S(1)}, s32[1,1,6]{2,1,0:T(1,128)}, u32[]{:S(2)}) copy-start(s32[1,1,6]{2,1,0:T(1,128)} %param.7) | copy-start | bytes 76
  3.4 11.2 %collective-permute-start = (f32[264,128]{1,0:T(8,128)}, f32[264,128]{1,0:T(8,128)S(1)}, u32[]{:S(2)}, u32[]{:S(2)}) collective-permute-start(f32[264,128]{1,0:T(8,128)} %get-tuple-element.28), channel_id=1, source_target_pairs={{0,1},{1,0},{2,4},{3,5},{4,2},{5,3},{6,8},{7,9},{8,6},{9,7},{10,12... | collective-permute-start | bytes 405512 | tf_op jit(solution)/shard_map/ppermute | solution.py:63
  6.4 8.1 %collective-permute-start.1 = (f32[264,128]{1,0:T(8,128)}, f32[264,128]{1,0:T(8,128)S(1)}, u32[]{:S(2)}, u32[]{:S(2)}) collective-permute-start(f32[264,128]{1,0:T(8,128)} %get-tuple-element.29), channel_id=1, source_target_pairs={{0,1},{1,0},{2,3},{3,2},{4,5},{5,4},{6,7},{7,6},{8,9},{9,8},{10,11... | collective-permute-start | bytes 405512 | tf_op jit(solution)/shard_map/ppermute | solution.py:63
  6.5 8.0 %collective-permute-start.2 = (f32[264,128]{1,0:T(8,128)}, f32[264,128]{1,0:T(8,128)S(1)}, u32[]{:S(2)}, u32[]{:S(2)}) collective-permute-start(f32[264,128]{1,0:T(8,128)} %get-tuple-element.30), channel_id=1, source_target_pairs={{0,2},{1,3},{2,0},{3,1},{4,6},{5,7},{6,4},{7,5},{8,10},{9,11},{10,... | collective-permute-start | bytes 405512 | tf_op jit(solution)/shard_map/ppermute | solution.py:63
  7.8 6.8 %copy-start.2 = (s32[1,1,6]{2,1,0:T(1,128)S(1)}, s32[1,1,6]{2,1,0:T(1,128)}, u32[]{:S(2)}) copy-start(s32[1,1,6]{2,1,0:T(1,128)} %param.6) | copy-start | bytes 76
  12.4 16.4 %collective-permute-start.3 = (f32[256,128]{1,0:T(8,128)S(1)}, f32[256,128]{1,0:T(8,128)S(1)}, u32[]{:S(2)}, u32[]{:S(2)}) collective-permute-start(f32[256,128]{1,0:T(8,128)S(1)} %get-tuple-element.33), channel_id=1, source_target_pairs={{0,1},{1,0},{2,4},{3,5},{4,2},{5,3},{6,8},{7,9},{8,6},{9,7},{10,12... | collective-permute-start | bytes 393224 | tf_op jit(solution)/shard_map/ppermute | solution.py:63
  13.2 15.6 %collective-permute-start.4 = (f32[256,128]{1,0:T(8,128)S(1)}, f32[256,128]{1,0:T(8,128)S(1)}, u32[]{:S(2)}, u32[]{:S(2)}) collective-permute-start(f32[256,128]{1,0:T(8,128)S(1)} %get-tuple-element.34), channel_id=1, source_target_pairs={{0,1},{1,0},{2,3},{3,2},{4,5},{5,4},{6,7},{7,6},{8,9},{9,8},{10,11... | collective-permute-start | bytes 393224 | tf_op jit(solution)/shard_map/ppermute | solution.py:63
  14.5 14.3 %collective-permute-start.5 = (f32[256,128]{1,0:T(8,128)S(1)}, f32[256,128]{1,0:T(8,128)S(1)}, u32[]{:S(2)}, u32[]{:S(2)}) collective-permute-start(f32[256,128]{1,0:T(8,128)S(1)} %get-tuple-element.35), channel_id=1, source_target_pairs={{0,2},{1,3},{2,0},{3,1},{4,6},{5,7},{6,4},{7,5},{8,10},{9,11},{10,... | collective-permute-start | bytes 393224 | tf_op jit(solution)/shard_map/ppermute | solution.py:63
  33.8 6.0 %collective-permute-start.7 = (f32[256,128]{1,0:T(8,128)S(1)}, f32[256,128]{1,0:T(8,128)S(1)}, u32[]{:S(2)}, u32[]{:S(2)}) collective-permute-start(f32[256,128]{1,0:T(8,128)S(1)} %more0.3.rest_5_), channel_id=1, source_target_pairs={{0,1},{1,0},{2,3},{3,2},{4,5},{5,4},{6,7},{7,6},{8,9},{9,8},{10,11... | collective-permute-start | bytes 393224 | tf_op jit(solution)/shard_map/ppermute | solution.py:63
  35.3 4.5 %collective-permute-start.8 = (f32[256,128]{1,0:T(8,128)S(1)}, f32[256,128]{1,0:T(8,128)S(1)}, u32[]{:S(2)}, u32[]{:S(2)}) collective-permute-start(f32[256,128]{1,0:T(8,128)S(1)} %more0.4.rest_6_), channel_id=1, source_target_pairs={{0,2},{1,3},{2,0},{3,1},{4,6},{5,7},{6,4},{7,5},{8,10},{9,11},{10,... | collective-permute-start | bytes 393224 | tf_op jit(solution)/shard_map/ppermute | solution.py:63
  35.3 5.9 %collective-permute-start.6 = (f32[256,128]{1,0:T(8,128)S(1)}, f32[256,128]{1,0:T(8,128)S(1)}, u32[]{:S(2)}, u32[]{:S(2)}) collective-permute-start(f32[256,128]{1,0:T(8,128)S(1)} %get-tuple-element.36.rest_4_), channel_id=1, source_target_pairs={{0,1},{1,0},{2,4},{3,5},{4,2},{5,3},{6,8},{7,9},{8,6},{9,7},{10,12... | collective-permute-start | bytes 393224 | tf_op jit(solution)/shard_map/ppermute | solution.py:63
  46.6 5.0 %collective-permute-start.10 = (f32[256,128]{1,0:T(8,128)S(1)}, f32[256,128]{1,0:T(8,128)S(1)}, u32[]{:S(2)}, u32[]{:S(2)}) collective-permute-start(f32[256,128]{1,0:T(8,128)S(1)} %more1.3.rest_1_), channel_id=1, source_target_pairs={{0,1},{1,0},{2,3},{3,2},{4,5},{5,4},{6,7},{7,6},{8,9},{9,8},{10,11... | collective-permute-start | bytes 393224 | tf_op jit(solution)/shard_map/ppermute | solution.py:63
  47.6 4.1 %collective-permute-start.11 = (f32[256,128]{1,0:T(8,128)S(1)}, f32[256,128]{1,0:T(8,128)S(1)}, u32[]{:S(2)}, u32[]{:S(2)}) collective-permute-start(f32[256,128]{1,0:T(8,128)S(1)} %more1.4.rest_2_), channel_id=1, source_target_pairs={{0,2},{1,3},{2,0},{3,1},{4,6},{5,7},{6,4},{7,5},{8,10},{9,11},{10,... | collective-permute-start | bytes 393224 | tf_op jit(solution)/shard_map/ppermute | solution.py:63
  47.6 5.5 %collective-permute-start.9 = (f32[256,128]{1,0:T(8,128)S(1)}, f32[256,128]{1,0:T(8,128)S(1)}, u32[]{:S(2)}, u32[]{:S(2)}) collective-permute-start(f32[256,128]{1,0:T(8,128)S(1)} %get-tuple-element.43.rest_0_), channel_id=1, source_target_pairs={{0,1},{1,0},{2,4},{3,5},{4,2},{5,3},{6,8},{7,9},{8,6},{9,7},{10,12... | collective-permute-start | bytes 393224 | tf_op jit(solution)/shard_map/ppermute | solution.py:63
